TPU v7x, 128 devices: a whole 4x4x4 slice. The times are simulated.
128 devices in a mesh: face: 8 (over y, x_hi), lon: 16 (over z, x_lo, core).
Axes of the slice: x: 4 (x_hi: 2, x_lo: 2; x = x_hi * 2 + x_lo), y: 4, z: 4, core: 2. Of those that a mesh axis runs over, the one named last changes fastest.
Arguments:
- source: bfloat16 [4096, 8, 128], P(('face', 'lon')), may hold values from -6 to 6
- intersection_weight: bfloat16 [4096, 4, 128, 128], P(('face', 'lon')), may hold values from -0.5 to 0.5
- dest_tile: int32 [4096, 4], P(('face', 'lon')), may hold values from 0 to 127, all different within a row; in each aligned block of 32 rows (0 to 31, 32 to 63, ...) at most 2 rows name the same one
- dest_row: int32 [4096, 4], P(('face', 'lon')), may hold values from 0 to 63
- prior_state: bfloat16 [8, 256, 4096], P(None, 'face', 'lon'), may hold values from -6 to 6
- lift_weight: bfloat16 [8, 64], replicated, may hold values from -9 to 9
- kernel: bfloat16 [9, 64, 64], replicated, may hold values from -0.23570226 to 0.23570226
- readout_weights: bfloat16 [64, 8], replicated, may hold values from -0.75 to 0.75
Outputs:
- remapped_reference: bfloat16 [8, 256, 4096], P(None, 'face', 'lon')
- network_estimate: bfloat16 [8, 256, 4096], P(None, 'face', 'lon')
- grad_lift: float32 [8, 64], replicated
- grad_kernel: float32 [9, 64, 64], replicated
- grad_head: float32 [64, 8], replicated
Inputs may be any that keep to these rules, and one draw needn't show every extreme that they name: `dest_tile`: the 4 intersections of a source block name distinct devices; the source blocks of one device name one device at most 2 times, and exactly 2 times for some device.
All inputs are finite; a program needn't handle non-finite values.
Results may differ from a plain program's by a relative error of at most 0.0013.
The roundings to bfloat16 on the way count: a program that leaves them out, or rounds other values in their place, can miss the bound.
Values may be sent and summed in bfloat16 or wider, within the bound.
A program may use at most 128 MiB of HBM per device.

v0:
```python
import functools

import jax
import jax.numpy as jnp
from jax import lax
from jax.experimental import pallas as pl
from jax.experimental.pallas import tpu as pltpu
from jax.sharding import PartitionSpec as P

MESH = pl.DeviceIdType.MESH
F32, BF16, I32 = jnp.float32, jnp.bfloat16, jnp.int32
N_FACE, N_LON = 8, 16
N_DEV = N_FACE * N_LON
NT = (((1,), (1,)), ((), ()))
WEIGHT_CHUNKS = 4


def mm(a, b):
    return jnp.dot(a, b, preferred_element_type=F32)


def nt(a, b):
    return lax.dot_general(a, b, NT, preferred_element_type=F32)


def rc(rows, cols):
    return (
        lax.broadcasted_iota(I32, (rows, cols), 0),
        lax.broadcasted_iota(I32, (rows, cols), 1),
    )


def onehot(mask):
    return jnp.where(mask, 1.0, 0.0).astype(BF16)


def peer(index):
    return (index // N_LON, index % N_LON)


def step_kernel(
    src_hbm, wts_hbm, tile_hbm, row_hbm, prior_hbm, lift_hbm, kern_hbm, read_hbm,
    rem_ref, est_ref, tot_ref,
    src, wts, dtile, drow, prior, lift, kern, read,
    contrib, idx_v, idx_s, lab_out, lab_in, send, recv,
    er_out, ec_out, er_in, ec_in, p3, l3, wconv, fore, hid, dsl, arr1, arr2, sum1,
    tbuf,
    in_sem, w_sem, idx_sem, lab_ss, lab_rs, pay_ss, pay_rs,
    halo_ss, halo_rs, ar_ss, ar1_rs, ar2_rs,
):
    face = lax.axis_index("face")
    lon = lax.axis_index("lon")
    me = face * N_LON + lon

    small = [
        (tile_hbm, dtile), (row_hbm, drow), (prior_hbm, prior), (src_hbm, src),
        (lift_hbm, lift), (kern_hbm, kern), (read_hbm, read),
    ]
    loads = [pltpu.make_async_copy(a, b, in_sem.at[i]) for i, (a, b) in enumerate(small)]
    for c in loads:
        c.start()
    per = 32 // WEIGHT_CHUNKS
    wloads = [
        pltpu.make_async_copy(
            wts_hbm.at[pl.ds(i * per, per)], wts.at[pl.ds(i * per, per)], w_sem.at[i]
        )
        for i in range(WEIGHT_CHUNKS)
    ]
    for c in wloads:
        c.start()

    barrier = pltpu.get_barrier_semaphore()

    def greet(i, carry):
        other = lax.rem(me + i, N_DEV)
        pl.semaphore_signal(barrier, inc=1, device_id=peer(other), device_id_type=MESH)
        return carry

    lax.fori_loop(1, N_DEV, greet, 0)
    for c in loads:
        c.wait()

    pr, ps = rc(128, 32)
    expand = onehot(pr // 4 == ps)
    dcol4 = mm(expand, dtile[...].astype(F32).astype(BF16))
    rcol4 = mm(expand, drow[...].astype(F32).astype(BF16))
    r4, c4 = rc(128, 4)
    pick = r4 % 4 == c4
    dcol = jnp.sum(jnp.where(pick, dcol4, 0.0), axis=1, keepdims=True)
    lcol = jnp.sum(jnp.where(pick, rcol4, 0.0), axis=1, keepdims=True)
    ri, ci = rc(128, 128)
    diag = jnp.where(ri == ci, jnp.broadcast_to(dcol, (128, 128)), 0.0)
    dlane = jnp.sum(diag, axis=0, keepdims=True)
    same = (jnp.broadcast_to(dcol, (128, 128)) == dlane) & (ci < ri)
    rank = jnp.sum(jnp.where(same, 1.0, 0.0), axis=1, keepdims=True)
    pos = 2.0 * dcol + rank
    r2, c2 = rc(128, 256)
    hit = jnp.broadcast_to(pos, (128, 256)) == c2.astype(F32)
    index = jnp.sum(jnp.where(hit, r2.astype(F32), 0.0), axis=0, keepdims=True)
    idx_v[...] = index.astype(I32)
    idx_copy = pltpu.make_async_copy(idx_v, idx_s, idx_sem)
    idx_copy.start()
    slot = ((ci // 8) % 2).astype(F32)
    labels = jnp.where(
        jnp.broadcast_to(rank, (128, 128)) == slot,
        jnp.broadcast_to(lcol, (128, 128)) + 1.0,
        0.0,
    ).astype(BF16)
    owners = onehot(jnp.broadcast_to(dlane, (128, 128)) == ri.astype(F32))
    code = mm(owners, labels) - 1.0
    code = jnp.where(code < 0.0, -1.0, code * 8.0 + (ci % 8).astype(F32)).astype(I32)
    lab_out[...] = code.reshape(128, 1, 128)
    lab_in[pl.ds(me, 1)] = lab_out[pl.ds(me, 1)]

    r, c = rc(256, 256)
    perm = onehot((r // 8 == c % 32) & (r % 8 == c // 32))
    shift0 = onehot(r == c - 1)
    shift2 = onehot(r == c + 1)
    eye = onehot(r == c)
    pf = mm(perm, prior[...].reshape(256, 256))
    pb = pf.astype(BF16)
    p3[1, pl.ds(16, 256), :] = pb
    er_out[...] = jnp.concatenate([pf[0:8], pf[248:256]], axis=0).astype(BF16)
    r16, c16 = rc(16, 256)
    edge = onehot(((r16 == 0) & (c16 == 0)) | ((r16 == 1) & (c16 == 255)))
    ec_out[...] = nt(edge, pb).astype(BF16)

    pl.semaphore_wait(barrier, N_DEV - 1)

    up, down = lax.rem(face + N_FACE - 1, N_FACE), lax.rem(face + 1, N_FACE)
    left, right = lax.rem(lon + N_LON - 1, N_LON), lax.rem(lon + 1, N_LON)
    halos = []
    ways = [(up, left), (up, lon), (up, right), (down, left), (down, lon), (down, right)]
    for k, (f, l) in enumerate(ways):
        halos.append(
            pltpu.make_async_remote_copy(
                er_out, er_in.at[5 - k], halo_ss.at[k], halo_rs.at[5 - k],
                device_id=(f, l), device_id_type=MESH,
            )
        )
    for k, l in enumerate((left, right)):
        halos.append(
            pltpu.make_async_remote_copy(
                ec_out, ec_in.at[1 - k], halo_ss.at[6 + k], halo_rs.at[7 - k],
                device_id=(face, l), device_id_type=MESH,
            )
        )
    for h in halos:
        h.start()

    def send_label(i, carry):
        other = lax.rem(me + i, N_DEV)
        pltpu.make_async_remote_copy(
            lab_out.at[other], lab_in.at[me], lab_ss, lab_rs,
            device_id=peer(other), device_id_type=MESH,
        ).start()
        return carry

    lax.fori_loop(1, N_DEV, send_label, 0)

    for chunk in range(WEIGHT_CHUNKS):
        wloads[chunk].wait()

        def regrid(s, carry):
            block = jnp.concatenate([wts[s, k] for k in range(4)], axis=1)
            out = mm(src[s], block)
            for k in range(4):
                contrib[s * 4 + k] = out[:, k * 128 : (k + 1) * 128].astype(BF16).astype(F32)
            return carry

        lax.fori_loop(chunk * per, (chunk + 1) * per, regrid, 0, unroll=4)
    idx_copy.wait()

    def place(d, carry):
        a = contrib[jnp.clip(idx_s[0, 2 * d], 0, 127)]
        b = contrib[jnp.clip(idx_s[0, 2 * d + 1], 0, 127)]
        send[d] = jnp.concatenate([a, b], axis=0).astype(BF16)
        return carry

    lax.fori_loop(0, N_DEV, place, 0, unroll=8)
    recv[pl.ds(me, 1)] = send[pl.ds(me, 1)]

    def send_block(i, carry):
        other = lax.rem(me + i, N_DEV)
        pltpu.make_async_remote_copy(
            send.at[other], recv.at[me], pay_ss, pay_rs,
            device_id=peer(other), device_id_type=MESH,
        ).start()
        return carry

    lax.fori_loop(1, N_DEV, send_block, 0)

    i64r, i64c = rc(128, 64)
    eye2 = onehot(i64r % 64 == i64c)
    liftf = lift[...].astype(F32)
    lift2 = jnp.concatenate([liftf, liftf], axis=0).astype(BF16)
    br, bc = rc(128, 16)
    block_mask = br // 64 == bc // 8
    bd_lift = jnp.where(block_mask, nt(eye2, lift2), 0.0).astype(BF16)
    read2 = jnp.concatenate([read[...], read[...]], axis=0)
    er8, ec8 = rc(8, 16)
    bd_read = jnp.where(block_mask, mm(read2, onehot(er8 == ec8 % 8)), 0.0).astype(BF16)
    fr8, fc8 = rc(16, 8)
    tr, tc = rc(16, 128)
    bd_read_t = jnp.where(
        tr // 8 == tc // 64, nt(onehot(fr8 % 8 == fc8), read2), 0.0
    ).astype(BF16)
    taps = kern[...].reshape(576, 64)
    zeros = jnp.zeros((192, 64), BF16)
    eye1 = eye2[0:64]
    wconv[0:64, :] = nt(eye1, jnp.concatenate([taps, zeros], axis=0)).astype(BF16)
    wconv[64:128, :] = nt(eye1, jnp.concatenate([zeros, taps], axis=0)).astype(BF16)

    for h in halos:
        h.wait()
    keep_up = jnp.where(face > 0, 1.0, 0.0)
    keep_down = jnp.where(face < N_FACE - 1, 1.0, 0.0)
    z8 = jnp.zeros((8, 256), F32)

    def rows_of(k):
        upper = er_in[k].astype(F32)[8:16] * keep_up
        lower = er_in[k + 3].astype(F32)[0:8] * keep_down
        return (
            jnp.concatenate([z8, upper], axis=0).astype(BF16),
            jnp.concatenate([lower, z8], axis=0).astype(BF16),
        )

    corner0 = onehot((r == 255) & (c == 0))
    corner2 = onehot((r == 0) & (c == 255))
    mid, lef, rig = rows_of(1), rows_of(0), rows_of(2)
    for at, e in ((0, 0), (272, 1)):
        p3[1, pl.ds(at, 16), :] = mid[e]
        p3[0, pl.ds(at, 16), :] = (mm(mid[e], shift0) + mm(lef[e], corner0)).astype(BF16)
        p3[2, pl.ds(at, 16), :] = (mm(mid[e], shift2) + mm(rig[e], corner2)).astype(BF16)
    col0 = onehot((r16 == 1) & (c16 == 0))
    col2 = onehot((r16 == 0) & (c16 == 255))
    from_left = nt(eye, ec_in[0]).astype(BF16)
    from_right = nt(eye, ec_in[1]).astype(BF16)
    p3[0, pl.ds(16, 256), :] = (mm(pb, shift0) + mm(from_left, col0)).astype(BF16)
    p3[2, pl.ds(16, 256), :] = (mm(pb, shift2) + mm(from_right, col2)).astype(BF16)

    def lift_pair(m, carry):
        at = pl.multiple_of(m * 16, 16)
        for j in range(3):
            out = mm(bd_lift, p3[j, pl.ds(at, 16), :]).astype(BF16)
            for e in range(2):
                to = pl.multiple_of((2 * m + e) * 192 + j * 64, 64)
                l3[pl.ds(to, 64), :] = out[e * 64 : (e + 1) * 64]
        return carry

    lax.fori_loop(0, 18, lift_pair, 0, unroll=2)

    def conv_pair(m, carry):
        at = pl.multiple_of((2 * m + 1) * 192, 64)
        act = mm(wconv[...], l3[pl.ds(at, 768), :])
        sig = 0.5 * jnp.tanh(0.5 * act) + 0.5
        hidden = (act * sig).astype(BF16)
        to = pl.multiple_of(m * 128, 128)
        hid[pl.ds(to, 128), :] = hidden
        dsl[pl.ds(to, 128), :] = sig * (1.0 + act * (1.0 - sig))
        row = pl.multiple_of(m * 16, 16)
        prow = pl.multiple_of(m * 16 + 16, 16)
        fore[pl.ds(row, 16), :] = p3[1, pl.ds(prow, 16), :].astype(F32) + mm(bd_read_t, hidden)
        return carry

    lax.fori_loop(0, 16, conv_pair, 0, unroll=2)
    perm_t = onehot((r // 32 == c % 8) & (r % 32 == c // 8))
    forecast = fore[...]
    est_ref[...] = mm(perm_t, forecast.astype(BF16)).astype(BF16).reshape(8, 32, 256)

    pltpu.make_async_copy(
        lab_in.at[pl.ds(0, N_DEV - 1)], lab_in.at[pl.ds(0, N_DEV - 1)], lab_rs
    ).wait()
    pltpu.make_async_copy(
        recv.at[pl.ds(0, N_DEV - 1)], recv.at[pl.ds(0, N_DEV - 1)], pay_rs
    ).wait()
    target = 16 * (r // 8) + r % 8
    halves = [jnp.zeros((256, 128), F32), jnp.zeros((256, 128), F32)]
    for t in range(8):
        lab = lab_in[pl.ds(16 * t, 16)].reshape(16, 128)
        lab = jnp.concatenate([lab, lab], axis=1)
        lane_code = jnp.sum(jnp.where(c16 // 16 == r16, lab, 0), axis=0, keepdims=True)
        lane_code = jnp.broadcast_to(lane_code, (256, 256))
        block = recv[pl.ds(16 * t, 16)].reshape(256, 128)
        for h in range(2):
            halves[h] = halves[h] + mm(onehot(lane_code == target + 8 * h), block)
    remap = jnp.concatenate(halves, axis=1).astype(BF16)
    rem_ref[...] = mm(perm_t, remap).astype(BF16).reshape(8, 32, 256)
    misfit = ((forecast - remap.astype(F32)) * (1.0 / 1024.0)).astype(BF16)
    fore[...] = misfit.astype(F32)

    def grad_pair(m, carry):
        head, accs = carry
        at = pl.multiple_of(m * 16, 16)
        to = pl.multiple_of(m * 128, 128)
        mis = fore[pl.ds(at, 16), :].astype(BF16)
        slope = (mm(bd_read, mis) * dsl[pl.ds(to, 128), :]).astype(BF16)
        head = head + nt(mis, hid[pl.ds(to, 128), :])
        accs = tuple(accs[j] + nt(p3[j, pl.ds(at, 48), :], slope) for j in range(3))
        return head, accs

    head, accs = lax.fori_loop(
        0, 16, grad_pair,
        (jnp.zeros((16, 128), F32), tuple(jnp.zeros((48, 128), F32) for _ in range(3))),
        unroll=2,
    )
    pairs = []
    for t in range(9):
        i, j = divmod(t, 3)
        pairs.append((accs[j][8 * i + 8 : 8 * i + 16], accs[j][8 * i + 16 : 8 * i + 24]))
    pairs.append((head[0:8], head[8:16]))
    low = lax.broadcasted_iota(I32, (8, 128), 1) < 64
    parts = []
    for b in range(5):
        a0, b0 = pairs[b]
        a1, b1 = pairs[b + 5]
        parts.append(
            jnp.where(low, a0 + pltpu.roll(b0, 64, 1), pltpu.roll(a1, 64, 1) + b1)
        )
    mine = jnp.concatenate(parts, axis=0)
    tbuf[...] = mine
    arr1[pl.ds(lon, 1)] = mine[None]

    def reduce_lon(i, carry):
        other = lax.rem(lon + i, N_LON)
        pltpu.make_async_remote_copy(
            tbuf, arr1.at[lon], ar_ss.at[0], ar1_rs,
            device_id=(face, other), device_id_type=MESH,
        ).start()
        return carry

    lax.fori_loop(1, N_LON, reduce_lon, 0)
    pltpu.make_async_copy(
        arr1.at[pl.ds(0, N_LON - 1)], arr1.at[pl.ds(0, N_LON - 1)], ar1_rs
    ).wait()
    total = arr1[0]
    for k in range(1, N_LON):
        total = total + arr1[k]
    sum1[...] = total
    arr2[pl.ds(face, 1)] = total[None]

    def reduce_face(i, carry):
        other = lax.rem(face + i, N_FACE)
        pltpu.make_async_remote_copy(
            sum1, arr2.at[face], ar_ss.at[1], ar2_rs,
            device_id=(other, lon), device_id_type=MESH,
        ).start()
        return carry

    lax.fori_loop(1, N_FACE, reduce_face, 0)
    pltpu.make_async_copy(
        arr2.at[pl.ds(0, N_FACE - 1)], arr2.at[pl.ds(0, N_FACE - 1)], ar2_rs
    ).wait()
    total = arr2[0]
    for k in range(1, N_FACE):
        total = total + arr2[k]
    tot_ref[...] = total

    pltpu.make_async_copy(
        lab_out.at[pl.ds(0, N_DEV - 1)], lab_out.at[pl.ds(0, N_DEV - 1)], lab_ss
    ).wait()
    pltpu.make_async_copy(
        send.at[pl.ds(0, N_DEV - 1)], send.at[pl.ds(0, N_DEV - 1)], pay_ss
    ).wait()
    pltpu.make_async_copy(
        arr1.at[pl.ds(0, N_LON - 1)], arr1.at[pl.ds(0, N_LON - 1)], ar_ss.at[0]
    ).wait()
    pltpu.make_async_copy(
        arr2.at[pl.ds(0, N_FACE - 1)], arr2.at[pl.ds(0, N_FACE - 1)], ar_ss.at[1]
    ).wait()


def final_kernel(tot, rem, est, lift, kern, rem_out, est_out, gl_out, gk_out, gh_out):
    rem_out[...] = rem[...]
    est_out[...] = est[...]

    def split(x):
        a = x.astype(BF16)
        x = x - a.astype(F32)
        b = x.astype(BF16)
        x = x - b.astype(F32)
        return a, b, x.astype(BF16)

    blocks = []
    for b in range(10):
        v = tot[(b % 5) * 8 : (b % 5) * 8 + 8, :]
        if b >= 5:
            v = pltpu.roll(v, 64, 1)
        parts = [p.astype(F32) for p in split(v)]
        parts.append(jnp.zeros((8, 128), F32))
        blocks.append(jnp.concatenate(parts, axis=0).astype(BF16)[:, 0:64])
    er, ec = rc(64, 64)
    eye = onehot(er == ec)
    liftf = lift[...].astype(F32)
    lift4 = jnp.concatenate([liftf] * 4, axis=0).astype(BF16)
    lift_t = nt(eye, lift4).astype(BF16)
    grad_lift = jnp.zeros((32, 64), F32)
    for t in range(9):
        gk_out[t] = mm(lift_t, blocks[t])
        grad_lift = grad_lift + nt(blocks[t], kern[t])
    gl_out[...] = grad_lift[0:8] + grad_lift[8:16] + grad_lift[16:24]
    sr, sc = rc(32, 8)
    head = nt(eye, blocks[9]).astype(BF16)
    gh_out[...] = mm(head, onehot(sr % 8 == sc))


def per_device(source, weight, dest_tile, dest_row, prior, lift, kern, read):
    any_spec = pl.BlockSpec(memory_space=pl.ANY)
    vmem = pl.BlockSpec(memory_space=pltpu.VMEM)
    V = pltpu.VMEM
    DMA = pltpu.SemaphoreType.DMA
    rem, est, tot = pl.pallas_call(
        step_kernel,
        out_shape=(
            jax.ShapeDtypeStruct((8, 32, 256), BF16),
            jax.ShapeDtypeStruct((8, 32, 256), BF16),
            jax.ShapeDtypeStruct((40, 128), F32),
        ),
        in_specs=[any_spec] * 8,
        out_specs=(vmem, vmem, vmem),
        scratch_shapes=[
            V((32, 8, 128), BF16), V((32, 4, 128, 128), BF16), V((32, 4), I32), V((32, 4), I32),
            V((8, 32, 256), BF16), V((8, 64), BF16), V((9, 64, 64), BF16), V((64, 8), BF16),
            V((128, 8, 128), F32), V((1, 256), I32), pltpu.SMEM((1, 256), I32),
            V((128, 1, 128), I32), V((128, 1, 128), I32),
            V((128, 16, 128), BF16), V((128, 16, 128), BF16),
            V((16, 256), BF16), V((16, 256), BF16), V((6, 16, 256), BF16), V((2, 16, 256), BF16),
            V((3, 288, 256), BF16), V((36 * 192, 256), BF16), V((128, 768), BF16),
            V((256, 256), F32), V((2048, 256), BF16), V((2048, 256), F32),
            V((16, 40, 128), F32), V((8, 40, 128), F32), V((40, 128), F32), V((40, 128), F32),
            DMA((7,)), DMA((WEIGHT_CHUNKS,)), DMA, DMA, DMA, DMA, DMA,
            DMA((8,)), DMA((8,)), DMA((2,)), DMA, DMA,
        ],
        compiler_params=pltpu.CompilerParams(
            collective_id=0, has_side_effects=True, vmem_limit_bytes=40 << 20
        ),
        name="step",
    )(source, weight, dest_tile, dest_row, prior, lift, kern, read)
    rem, est, gl, gk, gh = pl.pallas_call(
        final_kernel,
        out_shape=(
            jax.ShapeDtypeStruct((8, 32, 256), BF16),
            jax.ShapeDtypeStruct((8, 32, 256), BF16),
            jax.ShapeDtypeStruct((8, 64), F32),
            jax.ShapeDtypeStruct((9, 64, 64), F32),
            jax.ShapeDtypeStruct((64, 8), F32),
        ),
        in_specs=[vmem] * 5,
        out_specs=(vmem,) * 5,
        name="final",
    )(tot, rem, est, lift, kern)
    return rem, est, gl, gk, gh


def solution(mesh):
    return jax.shard_map(
        per_device,
        mesh=mesh,
        in_specs=(
            P(("face", "lon"), None, None),
            P(("face", "lon"), None, None, None),
            P(("face", "lon"), None),
            P(("face", "lon"), None),
            P(None, "face", "lon"),
            P(),
            P(),
            P(),
        ),
        out_specs=(P(None, "face", "lon"), P(None, "face", "lon"), P(), P(), P()),
        check_vma=False,
    )
```

profile of v0, /device:TPU:1, one launch (start us, length us, event | category | flops | bytes accessed | tf_op | source)
XLA Modules:
  0.0 56.8 jit_solution(4566648538632704961)
XLA Ops:
  0.6 0.8 %copy.13.tile_hbm = s32[32,4]{1,0:T(8,128)S(1)} copy(s32[32,4]{0,1:T(4,128)} %param.10) | data formatting | bytes 1024 | tf_op args[2]
  1.4 0.8 %copy.14.row_hbm = s32[32,4]{1,0:T(8,128)S(1)} copy(s32[32,4]{0,1:T(4,128)} %param.11) | data formatting | bytes 1024 | tf_op args[3]
  2.2 0.8 %copy.15.read_hbm = bf16[64,8]{1,0:T(8,128)(2,1)S(1)} copy(bf16[64,8]{0,1:T(8,128)(2,1)} %param.15) | data formatting | bytes 2048 | tf_op args[7]
  2.9 0.0 copy-start
  2.9 2.2 %copy-done = bf16[32,4,128,128]{3,2,1,0:T(8,128)(2,1)S(1)} copy-done((bf16[32,4,128,128]{3,2,1,0:T(8,128)(2,1)S(1)}, bf16[32,4,128,128]{3,2,1,0:T(8,128)(2,1)}, u32[]{:S(2)}) %copy-start) | copy-done | bytes 4194328
  5.1 0.0 copy-start.1
  5.1 0.9 %copy-done.1 = bf16[9,64,64]{2,1,0:T(8,128)(2,1)S(1)} copy-done((bf16[9,64,64]{2,1,0:T(8,128)(2,1)S(1)}, bf16[9,64,64]{2,1,0:T(8,128)(2,1)}, u32[]{:S(2)}) %copy-start.1) | copy-done | bytes 73752
  6.0 0.0 copy-start.2
  6.0 0.9 %copy-done.2 = bf16[8,32,256]{2,1,0:T(8,128)(2,1)S(1)} copy-done((bf16[8,32,256]{2,1,0:T(8,128)(2,1)S(1)}, bf16[8,32,256]{2,1,0:T(8,128)(2,1)}, u32[]{:S(2)}) %copy-start.2) | copy-done | bytes 131096
  6.9 0.0 copy-start.5
  6.9 0.8 %copy-done.5 = bf16[32,8,128]{2,1,0:T(8,128)(2,1)S(1)} copy-done((bf16[32,8,128]{2,1,0:T(8,128)(2,1)S(1)}, bf16[32,8,128]{2,1,0:T(8,128)(2,1)}, u32[]{:S(2)}) %copy-start.5) | copy-done | bytes 65560
  7.8 0.0 copy-start.7
  7.8 0.7 %copy-done.7 = bf16[8,64]{1,0:T(8,128)(2,1)S(1)} copy-done((bf16[8,64]{1,0:T(8,128)(2,1)S(1)}, bf16[8,64]{1,0:T(8,128)(2,1)}, u32[]{:S(2)}) %copy-start.7) | copy-done | bytes 1048
  8.5 42.8 %step.1 = (bf16[8,32,256]{2,1,0:T(8,128)(2,1)S(1)}, bf16[8,32,256]{2,1,0:T(8,128)(2,1)S(1)}, f32[40,128]{1,0:T(8,128)S(1)}) custom-call(bf16[32,8,128]{2,1,0:T(8,128)(2,1)S(1)} %copy-done.5, bf16[32,4,128,128]{3,2,1,0:T(8,128)(2,1)S(1)} %copy-done, s32[32,4]{1,0:T(8,128)S(1)} %copy.13.tile_hbm, s32[32,4]{1,0:T(8,128)S(1)} %copy.14.row_hbm, ...), custom_call_target="tpu_custom_call" | custom-call | tf_op jit(solution)/shard_map/step/pallas_call | solution.py:412
  51.3 0.0 copy-start.3
  51.3 0.6 %copy-done.3 = bf16[8,32,256]{2,1,0:T(8,128)(2,1)} copy-done((bf16[8,32,256]{2,1,0:T(8,128)(2,1)}, bf16[8,32,256]{2,1,0:T(8,128)(2,1)S(1)}, u32[]{:S(2)}) %copy-start.3) | copy-done | bytes 131096
  51.9 0.0 copy-start.4
  51.9 0.7 %copy-done.4 = bf16[8,32,256]{2,1,0:T(8,128)(2,1)} copy-done((bf16[8,32,256]{2,1,0:T(8,128)(2,1)}, bf16[8,32,256]{2,1,0:T(8,128)(2,1)S(1)}, u32[]{:S(2)}) %copy-start.4) | copy-done | bytes 131096
  52.6 0.0 copy-start.6
  52.6 0.6 %copy-done.6 = f32[40,128]{1,0:T(8,128)} copy-done((f32[40,128]{1,0:T(8,128)}, f32[40,128]{1,0:T(8,128)S(1)}, u32[]{:S(2)}) %copy-start.6) | copy-done | bytes 20504
  53.2 2.2 %final.1 = (bf16[8,32,256]{2,1,0:T(8,128)(2,1)}, bf16[8,32,256]{2,1,0:T(8,128)(2,1)}, f32[8,64]{1,0:T(8,128)}, f32[9,64,64]{2,1,0:T(8,128)}, f32[64,8]{1,0:T(8,128)}) custom-call(f32[40,128]{1,0:T(8,128)} %copy-done.6, bf16[8,32,256]{2,1,0:T(8,128)(2,1)} %copy-done.3, bf16[8,32,256]{2,1,0:T(8,128)(2,1)} %copy-done.4, bf16[8,64]{1,0:T(8,128)(2,1)} %lift.1, ...), custom_call_target="tpu_custom_call" | custom-call | tf_op jit(solution)/shard_map/final/pallas_call | solution.py:439
  55.4 1.4 %copy.16 = f32[64,8]{0,1:T(8,128)} copy(f32[64,8]{1,0:T(8,128)} %get-tuple-element.15) | data formatting | bytes 4096 | tf_op jit(solution)/shard_map/final/pallas_call | solution.py:439
Async XLA Ops:
  2.9 2.2 %copy-start = (bf16[32,4,128,128]{3,2,1,0:T(8,128)(2,1)S(1)}, bf16[32,4,128,128]{3,2,1,0:T(8,128)(2,1)}, u32[]{:S(2)}) copy-start(bf16[32,4,128,128]{3,2,1,0:T(8,128)(2,1)} %wts_hbm.1) | copy-start | bytes 12582916
  5.1 0.9 %copy-start.1 = (bf16[9,64,64]{2,1,0:T(8,128)(2,1)S(1)}, bf16[9,64,64]{2,1,0:T(8,128)(2,1)}, u32[]{:S(2)}) copy-start(bf16[9,64,64]{2,1,0:T(8,128)(2,1)} %kern.1) | copy-start | bytes 221188
  6.0 0.9 %copy-start.2 = (bf16[8,32,256]{2,1,0:T(8,128)(2,1)S(1)}, bf16[8,32,256]{2,1,0:T(8,128)(2,1)}, u32[]{:S(2)}) copy-start(bf16[8,32,256]{2,1,0:T(8,128)(2,1)} %prior_hbm.1) | copy-start | bytes 393220
  6.9 0.8 %copy-start.5 = (bf16[32,8,128]{2,1,0:T(8,128)(2,1)S(1)}, bf16[32,8,128]{2,1,0:T(8,128)(2,1)}, u32[]{:S(2)}) copy-start(bf16[32,8,128]{2,1,0:T(8,128)(2,1)} %src_hbm.1) | copy-start | bytes 196612
  7.8 0.7 %copy-start.7 = (bf16[8,64]{1,0:T(8,128)(2,1)S(1)}, bf16[8,64]{1,0:T(8,128)(2,1)}, u32[]{:S(2)}) copy-start(bf16[8,64]{1,0:T(8,128)(2,1)} %lift.1) | copy-start | bytes 3076
  51.3 0.6 %copy-start.3 = (bf16[8,32,256]{2,1,0:T(8,128)(2,1)}, bf16[8,32,256]{2,1,0:T(8,128)(2,1)S(1)}, u32[]{:S(2)}) copy-start(bf16[8,32,256]{2,1,0:T(8,128)(2,1)S(1)} %get-tuple-element.9.rem) | copy-start | bytes 393220
  51.9 0.7 %copy-start.4 = (bf16[8,32,256]{2,1,0:T(8,128)(2,1)}, bf16[8,32,256]{2,1,0:T(8,128)(2,1)S(1)}, u32[]{:S(2)}) copy-start(bf16[8,32,256]{2,1,0:T(8,128)(2,1)S(1)} %get-tuple-element.10.est) | copy-start | bytes 393220
  52.6 0.6 %copy-start.6 = (f32[40,128]{1,0:T(8,128)}, f32[40,128]{1,0:T(8,128)S(1)}, u32[]{:S(2)}) copy-start(f32[40,128]{1,0:T(8,128)S(1)} %get-tuple-element.8.tot) | copy-start | bytes 61444
where the time goes:
time: 57.3 us; the launch traced here: 56.8 us
  Pallas kernels  45 us (79%)
  local copies, waits for them, and re-layouts  11.1 us (19%)
  between operations  0.66 us (1%)
    pallas_call x1, Pallas kernels, per_device(): pl.pallas_call(step_kernel, out_shape=(jax.ShapeDtypeStruct((8, 32, 256),...  42.8 us
    unnamed x19, local copies, waits for them, and re-layouts  9.71 us
    pallas_call x1, Pallas kernels, per_device(): pl.pallas_call(final_kernel, out_shape=(jax.ShapeDtypeStruct((8, 32, 256)...  2.2 us
    pallas_call x1, local copies, waits for them, and re-layouts, per_device(): pl.pallas_call(final_kernel, out_shape=(jax.ShapeDtypeStruct((8, 32, 256)...  1.42 us

commit v1 on v0

v1 whole, which is shorter than its diff:
```python
import jax
import jax.numpy as jnp
from jax import lax
from jax.experimental import pallas as pl
from jax.experimental.pallas import tpu as pltpu
from jax.sharding import PartitionSpec as P

MESH, LOGICAL = pl.DeviceIdType.MESH, pl.DeviceIdType.LOGICAL
F32, BF16, I32 = jnp.float32, jnp.bfloat16, jnp.int32
N_FACE, N_LON = 8, 16
N_DEV = N_FACE * N_LON
NT = (((1,), (1,)), ((), ()))
WEIGHT_CHUNKS = 4
LIFT_UNROLL, CONV_UNROLL, GRAD_UNROLL = 3, 2, 2


def mm(a, b):
    return jnp.dot(a, b, preferred_element_type=F32)


def nt(a, b):
    return lax.dot_general(a, b, NT, preferred_element_type=F32)


def rc(rows, cols):
    return (
        lax.broadcasted_iota(I32, (rows, cols), 0),
        lax.broadcasted_iota(I32, (rows, cols), 1),
    )


def onehot(mask):
    return jnp.where(mask, 1.0, 0.0).astype(BF16)


def step_kernel(
    src_hbm, wts_hbm, tile_hbm, row_hbm, prior_hbm, lift_hbm, kern_hbm, read_hbm,
    rem_ref, est_ref, tot_ref,
    src, wts, dtile, drow, prior, lift, kern, read,
    contrib, idx_v, idx_s, lab_out, lab_in, send, recv, wide,
    er_out, ec_out, er_in, ec_in, p3, l3, wconv, fore, mis_ref, hid, dsl, arr1, arr2, sum1,
    tbuf,
    in_sem, w_sem, idx_sem, lab_ss, lab_rs, pay_ss, pay_rs,
    halo_ss, halo_rs, ar_ss, ar1_rs, ar2_rs,
):
    face = lax.axis_index("face")
    lon = lax.axis_index("lon")
    me = face * N_LON + lon

    small = [
        (tile_hbm, dtile), (row_hbm, drow), (prior_hbm, prior), (src_hbm, src),
        (lift_hbm, lift), (kern_hbm, kern), (read_hbm, read),
    ]
    loads = [pltpu.make_async_copy(a, b, in_sem.at[i]) for i, (a, b) in enumerate(small)]
    for c in loads:
        c.start()
    per = 32 // WEIGHT_CHUNKS
    wloads = [
        pltpu.make_async_copy(
            wts_hbm.at[pl.ds(i * per, per)], wts.at[pl.ds(i * per, per)], w_sem.at[i]
        )
        for i in range(WEIGHT_CHUNKS)
    ]
    for c in wloads:
        c.start()

    barrier = pltpu.get_barrier_semaphore()

    def others(action):
        def one(other):
            other = jnp.where(other == N_DEV - 1, 0, other + 1)
            action(other)
            return other

        other = me
        for _ in range(7):
            other = one(other)

        def eight(i, other):
            for _ in range(8):
                other = one(other)
            return other

        lax.fori_loop(1, N_DEV // 8, eight, other)

    others(
        lambda other: pl.semaphore_signal(
            barrier, inc=1, device_id=other, device_id_type=LOGICAL
        )
    )
    for c in loads:
        c.wait()

    ri, ci = rc(128, 128)
    tiles, rows = dtile[...], drow[...]
    d_row = jnp.concatenate([tiles[k : k + 1] for k in range(4)], axis=1)
    l_row = jnp.concatenate([rows[k : k + 1] for k in range(4)], axis=1)
    d_mat = jnp.broadcast_to(d_row, (128, 128))
    d_col = d_mat.T
    rank = jnp.sum(jnp.where((d_col == d_mat) & (ri < ci), 1, 0), axis=0, keepdims=True)
    pos = jnp.broadcast_to(2 * d_row + rank, (128, 128)).T
    idx_v[...] = jnp.concatenate(
        [
            jnp.sum(jnp.where(pos == ci + at, ri, 0), axis=0, keepdims=True)
            for at in (0, 128)
        ],
        axis=1,
    )
    idx_copy = pltpu.make_async_copy(idx_v, idx_s, idx_sem)
    idx_copy.start()
    l_col = jnp.broadcast_to(l_row, (128, 128)).T
    labels = jnp.where(pos - 2 * d_col == ci % 2, l_col + 1, 0).astype(F32).astype(BF16)
    code = (mm(onehot(d_mat == ri), labels) - 1.0).astype(I32)
    lab_out[...] = code.reshape(128, 1, 128)
    lab_in[pl.ds(me, 1)] = lab_out[pl.ds(me, 1)]

    r, c = rc(256, 256)
    perm = onehot((r // 8 == c % 32) & (r % 8 == c // 32))
    shift0 = onehot(r == c - 1)
    shift2 = onehot(r == c + 1)
    eye = onehot(r == c)
    pf = mm(perm, prior[...].reshape(256, 256))
    pb = pf.astype(BF16)
    p3[1, pl.ds(16, 256), :] = pb
    er_out[...] = jnp.concatenate([pf[0:8], pf[248:256]], axis=0).astype(BF16)
    r16, c16 = rc(16, 256)
    edge = onehot(((r16 == 0) & (c16 == 0)) | ((r16 == 1) & (c16 == 255)))
    ec_out[...] = nt(edge, pb).astype(BF16)

    i64r, i64c = rc(128, 64)
    eye2 = onehot(i64r % 64 == i64c)
    liftf = lift[...].astype(F32)
    lift2 = jnp.concatenate([liftf, liftf], axis=0).astype(BF16)
    br, bc = rc(128, 16)
    block_mask = br // 64 == bc // 8
    bd_lift = jnp.where(block_mask, nt(eye2, lift2), 0.0).astype(BF16)
    readf = read[...].astype(F32)
    read2 = jnp.concatenate([readf, readf], axis=0).astype(BF16)
    bd_read = jnp.where(block_mask, nt(eye2, read2), 0.0).astype(BF16)
    tr, tc = rc(16, 128)
    bd_read_t = jnp.where(
        tr // 8 == tc // 64,
        jnp.concatenate([jnp.concatenate([readf, readf], axis=1)] * 2, axis=0),
        0.0,
    ).astype(BF16)
    taps = kern[...].reshape(576, 64)
    zeros = jnp.zeros((192, 64), BF16)
    eye1 = eye2[0:64]
    wconv[0:64, :] = nt(eye1, jnp.concatenate([taps, zeros], axis=0)).astype(BF16)
    wconv[64:128, :] = nt(eye1, jnp.concatenate([zeros, taps], axis=0)).astype(BF16)

    for chunk in range(WEIGHT_CHUNKS):
        wloads[chunk].wait()

        def regrid(s, carry):
            block = jnp.concatenate([wts[s, k] for k in range(4)], axis=1)
            out = mm(src[s], block)
            for k in range(4):
                contrib[k * 32 + s] = out[:, k * 128 : (k + 1) * 128].astype(BF16).astype(F32)
            return carry

        lax.fori_loop(chunk * per, (chunk + 1) * per, regrid, 0, unroll=4)
    idx_copy.wait()

    def place(d, carry):
        a = contrib[idx_s[0, 2 * d]]
        b = contrib[idx_s[0, 2 * d + 1]]
        send[d] = jnp.concatenate([a, b], axis=0).astype(BF16)
        return carry

    lax.fori_loop(0, N_DEV, place, 0, unroll=16)
    recv[pl.ds(me, 1)] = send[pl.ds(me, 1)]

    pl.semaphore_wait(barrier, N_DEV - 1)

    up, down = lax.rem(face + N_FACE - 1, N_FACE), lax.rem(face + 1, N_FACE)
    left, right = lax.rem(lon + N_LON - 1, N_LON), lax.rem(lon + 1, N_LON)
    halos = []
    ways = [(up, left), (up, lon), (up, right), (down, left), (down, lon), (down, right)]
    for k, (f, l) in enumerate(ways):
        halos.append(
            pltpu.make_async_remote_copy(
                er_out, er_in.at[5 - k], halo_ss.at[k], halo_rs.at[5 - k],
                device_id=(f, l), device_id_type=MESH,
            )
        )
    for k, l in enumerate((left, right)):
        halos.append(
            pltpu.make_async_remote_copy(
                ec_out, ec_in.at[1 - k], halo_ss.at[6 + k], halo_rs.at[7 - k],
                device_id=(face, l), device_id_type=MESH,
            )
        )
    for h in halos:
        h.start()

    def send_block(other):
        pltpu.make_async_remote_copy(
            send.at[other], recv.at[me], pay_ss, pay_rs,
            device_id=other, device_id_type=LOGICAL,
        ).start()
        pltpu.make_async_remote_copy(
            lab_out.at[other], lab_in.at[me], lab_ss, lab_rs,
            device_id=other, device_id_type=LOGICAL,
        ).start()

    others(send_block)

    for h in halos:
        h.wait()
    keep_up = jnp.where(face > 0, 1.0, 0.0)
    keep_down = jnp.where(face < N_FACE - 1, 1.0, 0.0)
    z8 = jnp.zeros((8, 256), F32)

    def rows_of(k):
        upper = er_in[k].astype(F32)[8:16] * keep_up
        lower = er_in[k + 3].astype(F32)[0:8] * keep_down
        return jnp.concatenate([z8, upper, lower, z8], axis=0).astype(BF16)

    corner0 = onehot((r == 255) & (c == 0))
    corner2 = onehot((r == 0) & (c == 255))
    mid, lef, rig = rows_of(1), rows_of(0), rows_of(2)
    outer0 = (mm(mid, shift0) + mm(lef, corner0)).astype(BF16)
    outer2 = (mm(mid, shift2) + mm(rig, corner2)).astype(BF16)
    for j, outer in ((0, outer0), (1, mid), (2, outer2)):
        p3[j, pl.ds(0, 16), :] = outer[0:16]
        p3[j, pl.ds(272, 16), :] = outer[16:32]
    col0 = onehot((r16 == 1) & (c16 == 0))
    col2 = onehot((r16 == 0) & (c16 == 255))
    pb = p3[1, pl.ds(16, 256), :]
    from_left = nt(eye, ec_in[0]).astype(BF16)
    from_right = nt(eye, ec_in[1]).astype(BF16)
    p3[0, pl.ds(16, 256), :] = (mm(pb, shift0) + mm(from_left, col0)).astype(BF16)
    p3[2, pl.ds(16, 256), :] = (mm(pb, shift2) + mm(from_right, col2)).astype(BF16)

    def lift_pair(m, carry):
        at = pl.multiple_of(m * 16, 16)
        for j in range(3):
            out = mm(bd_lift, p3[j, pl.ds(at, 16), :]).astype(BF16)
            for e in range(2):
                to = pl.multiple_of((2 * m + e) * 192 + j * 64, 64)
                l3[pl.ds(to, 64), :] = out[e * 64 : (e + 1) * 64]
        return carry

    lax.fori_loop(0, 18, lift_pair, 0, unroll=LIFT_UNROLL)

    def conv_pair(m, carry):
        at = pl.multiple_of((2 * m + 1) * 192, 64)
        act = mm(wconv[...], l3[pl.ds(at, 768), :])
        sig = 0.5 * jnp.tanh(0.5 * act) + 0.5
        hidden = (act * sig).astype(BF16)
        to = pl.multiple_of(m * 128, 128)
        hid[pl.ds(to, 128), :] = hidden
        dsl[pl.ds(to, 128), :] = sig * (1.0 + act * (1.0 - sig))
        row = pl.multiple_of(m * 16, 16)
        prow = pl.multiple_of(m * 16 + 16, 16)
        fore[pl.ds(row, 16), :] = p3[1, pl.ds(prow, 16), :].astype(F32) + mm(bd_read_t, hidden)
        return carry

    lax.fori_loop(0, 16, conv_pair, 0, unroll=CONV_UNROLL)
    perm_t = onehot((r // 32 == c % 8) & (r % 32 == c // 8))
    est_ref[...] = mm(perm_t, fore[...].astype(BF16)).astype(BF16).reshape(8, 32, 256)

    pltpu.make_async_copy(
        lab_in.at[pl.ds(0, N_DEV - 1)], lab_in.at[pl.ds(0, N_DEV - 1)], lab_rs
    ).wait()
    lab = lab_in[...].reshape(128, 128)
    lr, lc = rc(64, 128)
    mine_mask = lr == lc // 2
    lane_label = jnp.concatenate(
        [
            jnp.sum(jnp.where(mine_mask, lab[at : at + 64], 0), axis=0, keepdims=True)
            for at in (0, 64)
        ],
        axis=1,
    )
    hr, _ = rc(64, 256)
    picker = onehot(jnp.broadcast_to(lane_label, (64, 256)) == 2 * (hr % 32) + hr // 32)
    pltpu.make_async_copy(
        recv.at[pl.ds(0, N_DEV - 1)], recv.at[pl.ds(0, N_DEV - 1)], pay_rs
    ).wait()
    wide[...] = recv[...].reshape(2048, 128).astype(F32)
    fields = []
    for q in range(8):
        block = wide[pl.ds(q, 256, stride=8), :].astype(BF16)
        part = mm(picker, block)
        fields.append(jnp.concatenate([part[0:32], part[32:64]], axis=1).astype(BF16))
    for q in range(8):
        rem_ref[q] = fields[q]
    remap = mm(perm, jnp.concatenate(fields, axis=0))
    mis_ref[...] = ((fore[...] - remap) * (1.0 / 1024.0)).astype(BF16)

    def grad_pair(m, carry):
        head, acc = carry
        at = pl.multiple_of(m * 16, 16)
        to = pl.multiple_of(m * 128, 128)
        mis = mis_ref[pl.ds(at, 16), :]
        slope = (mm(bd_read, mis) * dsl[pl.ds(to, 128), :]).astype(BF16)
        head = head + nt(mis, hid[pl.ds(to, 128), :])
        window = jnp.concatenate([p3[j, pl.ds(at, 48), :] for j in range(3)], axis=0)
        return head, acc + nt(window, slope)

    head, acc = lax.fori_loop(
        0, 16, grad_pair,
        (jnp.zeros((16, 128), F32), jnp.zeros((144, 128), F32)),
        unroll=GRAD_UNROLL,
    )
    pairs = []
    for t in range(9):
        i, j = divmod(t, 3)
        at = 48 * j + 8 * i + 8
        pairs.append((acc[at : at + 8], acc[at + 8 : at + 16]))
    pairs.append((head[0:8], head[8:16]))
    low = lax.broadcasted_iota(I32, (8, 128), 1) < 64
    parts = []
    for b in range(5):
        a0, b0 = pairs[b]
        a1, b1 = pairs[b + 5]
        parts.append(
            jnp.where(low, a0 + pltpu.roll(b0, 64, 1), pltpu.roll(a1, 64, 1) + b1)
        )
    mine = jnp.concatenate(parts, axis=0)
    tbuf[...] = mine
    arr1[pl.ds(lon, 1)] = mine[None]
    for i in range(1, N_LON):
        pltpu.make_async_remote_copy(
            tbuf, arr1.at[lon], ar_ss.at[0], ar1_rs,
            device_id=(face, lax.rem(lon + i, N_LON)), device_id_type=MESH,
        ).start()
    pltpu.make_async_copy(
        arr1.at[pl.ds(0, N_LON - 1)], arr1.at[pl.ds(0, N_LON - 1)], ar1_rs
    ).wait()
    total = arr1[0]
    for k in range(1, N_LON):
        total = total + arr1[k]
    sum1[...] = total
    arr2[pl.ds(face, 1)] = total[None]
    for i in range(1, N_FACE):
        pltpu.make_async_remote_copy(
            sum1, arr2.at[face], ar_ss.at[1], ar2_rs,
            device_id=(lax.rem(face + i, N_FACE), lon), device_id_type=MESH,
        ).start()
    pltpu.make_async_copy(
        arr2.at[pl.ds(0, N_FACE - 1)], arr2.at[pl.ds(0, N_FACE - 1)], ar2_rs
    ).wait()
    total = arr2[0]
    for k in range(1, N_FACE):
        total = total + arr2[k]
    tot_ref[...] = total

    pltpu.make_async_copy(
        lab_out.at[pl.ds(0, N_DEV - 1)], lab_out.at[pl.ds(0, N_DEV - 1)], lab_ss
    ).wait()
    pltpu.make_async_copy(
        send.at[pl.ds(0, N_DEV - 1)], send.at[pl.ds(0, N_DEV - 1)], pay_ss
    ).wait()
    pltpu.make_async_copy(
        arr1.at[pl.ds(0, N_LON - 1)], arr1.at[pl.ds(0, N_LON - 1)], ar_ss.at[0]
    ).wait()
    pltpu.make_async_copy(
        arr2.at[pl.ds(0, N_FACE - 1)], arr2.at[pl.ds(0, N_FACE - 1)], ar_ss.at[1]
    ).wait()


def final_kernel(
    tot_any, rem_any, est_any, lift, kern, rem_out, est_out, gl_out, gk_out, gh_out, tot, sem
):
    moves = [
        pltpu.make_async_copy(tot_any, tot, sem.at[0]),
        pltpu.make_async_copy(rem_any, rem_out, sem.at[1]),
        pltpu.make_async_copy(est_any, est_out, sem.at[2]),
    ]
    for m in moves:
        m.start()
    moves[0].wait()

    def split(x):
        a = x.astype(BF16)
        x = x - a.astype(F32)
        b = x.astype(BF16)
        x = x - b.astype(F32)
        return a, b, x.astype(BF16)

    blocks = []
    for b in range(10):
        v = tot[(b % 5) * 8 : (b % 5) * 8 + 8, :]
        if b >= 5:
            v = pltpu.roll(v, 64, 1)
        if b == 9:
            gh_out[...] = v[:, 0:64]
            break
        parts = [p.astype(F32) for p in split(v)]
        parts.append(jnp.zeros((8, 128), F32))
        blocks.append(jnp.concatenate(parts, axis=0).astype(BF16)[:, 0:64])
    er, ec = rc(64, 64)
    eye = onehot(er == ec)
    liftf = lift[...].astype(F32)
    lift4 = jnp.concatenate([liftf] * 4, axis=0).astype(BF16)
    lift_t = nt(eye, lift4).astype(BF16)
    grad_lift = jnp.zeros((32, 64), F32)
    for t in range(9):
        gk_out[t] = mm(lift_t, blocks[t])
        grad_lift = grad_lift + nt(blocks[t], kern[t])
    gl_out[...] = grad_lift[0:8] + grad_lift[8:16] + grad_lift[16:24]
    moves[1].wait()
    moves[2].wait()


def per_device(source, weight, dest_tile, dest_row, prior, lift, kern, read):
    any_spec = pl.BlockSpec(memory_space=pl.ANY)
    hbm = pl.BlockSpec(memory_space=pltpu.HBM)
    vmem = pl.BlockSpec(memory_space=pltpu.VMEM)
    V = pltpu.VMEM
    DMA = pltpu.SemaphoreType.DMA
    rem, est, tot = pl.pallas_call(
        step_kernel,
        out_shape=(
            jax.ShapeDtypeStruct((8, 32, 256), BF16),
            jax.ShapeDtypeStruct((8, 32, 256), BF16),
            jax.ShapeDtypeStruct((40, 128), F32),
        ),
        in_specs=[hbm] * 8,
        out_specs=(vmem, vmem, vmem),
        scratch_shapes=[
            V((32, 8, 128), BF16), V((32, 4, 128, 128), BF16), V((4, 32), I32), V((4, 32), I32),
            V((8, 32, 256), BF16), V((8, 64), BF16), V((9, 64, 64), BF16), V((8, 64), BF16),
            V((128, 8, 128), F32), V((1, 256), I32), pltpu.SMEM((1, 256), I32),
            V((128, 1, 128), I32), V((128, 1, 128), I32),
            V((128, 16, 128), BF16), V((128, 16, 128), BF16), V((2048, 128), F32),
            V((16, 256), BF16), V((16, 256), BF16), V((6, 16, 256), BF16), V((2, 16, 256), BF16),
            V((3, 288, 256), BF16), V((36 * 192, 256), BF16), V((128, 768), BF16),
            V((256, 256), F32), V((256, 256), BF16), V((2048, 256), BF16), V((2048, 256), F32),
            V((16, 40, 128), F32), V((8, 40, 128), F32), V((40, 128), F32), V((40, 128), F32),
            DMA((7,)), DMA((WEIGHT_CHUNKS,)), DMA, DMA, DMA, DMA, DMA,
            DMA((8,)), DMA((8,)), DMA((2,)), DMA, DMA,
        ],
        compiler_params=pltpu.CompilerParams(
            collective_id=0, has_side_effects=True, vmem_limit_bytes=40 << 20
        ),
        name="step",
    )(*(
        pltpu.with_memory_space_constraint(x, pltpu.HBM)
        for x in (source, weight, dest_tile.T, dest_row.T, prior, lift, kern, read.T)
    ))
    rem, est, gl, gk, gh = pl.pallas_call(
        final_kernel,
        out_shape=(
            jax.ShapeDtypeStruct((8, 32, 256), BF16),
            jax.ShapeDtypeStruct((8, 32, 256), BF16),
            jax.ShapeDtypeStruct((8, 64), F32),
            jax.ShapeDtypeStruct((9, 64, 64), F32),
            jax.ShapeDtypeStruct((8, 64), F32),
        ),
        in_specs=[any_spec] * 3 + [vmem] * 2,
        out_specs=(hbm, hbm, vmem, vmem, vmem),
        scratch_shapes=[V((40, 128), F32), DMA((3,))],
        compiler_params=pltpu.CompilerParams(vmem_limit_bytes=16 << 20),
        name="final",
    )(tot, rem, est, lift, kern)
    return rem, est, gl, gk, gh.T


def solution(mesh):
    return jax.shard_map(
        per_device,
        mesh=mesh,
        in_specs=(
            P(("face", "lon"), None, None),
            P(("face", "lon"), None, None, None),
            P(("face", "lon"), None),
            P(("face", "lon"), None),
            P(None, "face", "lon"),
            P(),
            P(),
            P(),
        ),
        out_specs=(P(None, "face", "lon"), P(None, "face", "lon"), P(), P(), P()),
        check_vma=False,
    )
```

time: 57.3 us -> 39.1 us (0.68)
  local copies, waits for them, and re-layouts: 11.1 us -> 0.01 us
  Pallas kernels: 45 us -> 38.3 us
    unnamed x19 -> x4, local copies, waits for them, and re-layouts: 9.71 us -> 0.01 us
    pallas_call x1, Pallas kernels: 42.8 us -> 36.9 us  [per_device(): pl.pallas_call(step_kernel, out_shape=(jax.ShapeDtypeStruct((8, 32, 256),...]
    pallas_call x1 -> x0, local copies, waits for them, and re-layouts: 1.42 us -> none  [per_device(): pl.pallas_call(final_kernel, out_shape=(jax.ShapeDtypeStruct((8, 32, 256)...]
    pallas_call x1, Pallas kernels: 2.2 us -> 1.47 us  [per_device(): pl.pallas_call(final_kernel, out_shape=(jax.ShapeDtypeStruct((8, 32, 256)...]
where the time goes in v1:
time: 39.1 us; the launch traced here: 39 us
  Pallas kernels  38.3 us (98%)
  between operations  0.67 us (2%)
    pallas_call x1, Pallas kernels, per_device(): pl.pallas_call(step_kernel, out_shape=(jax.ShapeDtypeStruct((8, 32, 256),...  36.9 us
    pallas_call x1, Pallas kernels, per_device(): pl.pallas_call(final_kernel, out_shape=(jax.ShapeDtypeStruct((8, 32, 256)...  1.47 us

profile of v1, /device:TPU:1, one launch (start us, length us, event | category | flops | bytes accessed | tf_op | source)
XLA Modules:
  0.0 39.0 jit_solution(8614821966904856397)
XLA Ops:
  0.6 0.0 copy-start
  0.6 0.0 copy-start.1
  0.7 36.9 %step.1 = (bf16[8,32,256]{2,1,0:T(8,128)(2,1)S(1)}, bf16[8,32,256]{2,1,0:T(8,128)(2,1)S(1)}, f32[40,128]{1,0:T(8,128)S(1)}) custom-call(bf16[32,8,128]{2,1,0:T(8,128)(2,1)} %src_hbm.1, bf16[32,4,128,128]{3,2,1,0:T(8,128)(2,1)} %wts_hbm.1, s32[4,32]{1,0:T(4,128)} %bitcast.4, s32[4,32]{1,0:T(4,128)} %bitcast.5, bf16[8,32,256]{2,1,0:T(8,128)(2,1)} %prior_hbm.1, ...), custom_call_target="tpu_custom_call" | custom-call | tf_op jit(solution)/shard_map/step/pallas_call | solution.py:415
  37.5 0.0 copy-done
  37.6 0.0 copy-done.1
  37.6 1.5 %final.1 = (bf16[8,32,256]{2,1,0:T(8,128)(2,1)}, bf16[8,32,256]{2,1,0:T(8,128)(2,1)}, f32[8,64]{1,0:T(8,128)}, f32[9,64,64]{2,1,0:T(8,128)}, f32[8,64]{1,0:T(8,128)}) custom-call(f32[40,128]{1,0:T(8,128)S(1)} %get-tuple-element.13.tot_any, bf16[8,32,256]{2,1,0:T(8,128)(2,1)S(1)} %get-tuple-element.14.rem_any, ...), custom_call_target="tpu_custom_call" | custom-call | tf_op jit(solution)/shard_map/final/pallas_call | solution.py:445
Async XLA Ops:
  0.6 36.9 %copy-start = (bf16[9,64,64]{2,1,0:T(8,128)(2,1)S(1)}, bf16[9,64,64]{2,1,0:T(8,128)(2,1)}, u32[]{:S(2)}) copy-start(bf16[9,64,64]{2,1,0:T(8,128)(2,1)} %kern.1) | copy-start | bytes 221188
  0.6 36.9 %copy-start.1 = (bf16[8,64]{1,0:T(8,128)(2,1)S(1)}, bf16[8,64]{1,0:T(8,128)(2,1)}, u32[]{:S(2)}) copy-start(bf16[8,64]{1,0:T(8,128)(2,1)} %lift.1) | copy-start | bytes 3076

commit v2 on v1

--- a/solution.py
+++ b/solution.py
@@ -11,7 +11,7 @@
 N_DEV = N_FACE * N_LON
 NT = (((1,), (1,)), ((), ()))
 WEIGHT_CHUNKS = 4
-LIFT_UNROLL, CONV_UNROLL, GRAD_UNROLL = 3, 2, 2
+LIFT_UNROLL, CONV_UNROLL, GRAD_UNROLL = 3, 3, 8
 
 
 def mm(a, b):
@@ -38,7 +38,7 @@
     rem_ref, est_ref, tot_ref,
     src, wts, dtile, drow, prior, lift, kern, read,
     contrib, idx_v, idx_s, lab_out, lab_in, send, recv, wide,
-    er_out, ec_out, er_in, ec_in, p3, l3, wconv, fore, mis_ref, hid, dsl, arr1, arr2, sum1,
+    er_out, ec_out, er_in, ec_in, p3, l3, wconv, fore, mis_ref, hid, dsl, acts, arr1, arr2, sum1,
     tbuf,
     in_sem, w_sem, idx_sem, lab_ss, lab_rs, pay_ss, pay_rs,
     halo_ss, halo_rs, ar_ss, ar1_rs, ar2_rs,
@@ -46,7 +46,34 @@
     face = lax.axis_index("face")
     lon = lax.axis_index("lon")
     me = face * N_LON + lon
-
+    y, z = face // 2, lon // 4
+    x = (face % 2) * 2 + (lon // 2) % 2
+    core = lon % 2
+
+    def at_xc(x_at, core_at):
+        return (x_at // 2) * 16 + (x_at % 2) * 2 + core_at
+
+    barrier = pltpu.get_barrier_semaphore()
+
+    def others(action):
+        zc = []
+        for dz, dc in ((2, 1), (2, 0), (1, 1), (3, 1), (1, 0), (3, 0), (0, 1), (0, 0)):
+            zc.append((lax.rem(z + dz, 4) * 4 + lax.rem(core + dc, 2), (dz, dc)))
+        far = sorted(
+            ((dy, dx) for dy in range(4) for dx in range(4)),
+            key=lambda d: -(min(d[0], 4 - d[0]) + min(d[1], 4 - d[1])),
+        )
+        for dy, dx in far:
+            base = lax.rem(y + dy, 4) * 32 + at_xc(lax.rem(x + dx, 4), 0)
+            for offset, d in zc:
+                if (dy, dx) + d != (0, 0, 0, 0):
+                    action(base + offset)
+
+    others(
+        lambda other: pl.semaphore_signal(
+            barrier, inc=1, device_id=other, device_id_type=LOGICAL
+        )
+    )
     small = [
         (tile_hbm, dtile), (row_hbm, drow), (prior_hbm, prior), (src_hbm, src),
         (lift_hbm, lift), (kern_hbm, kern), (read_hbm, read),
@@ -64,30 +91,6 @@
     for c in wloads:
         c.start()
 
-    barrier = pltpu.get_barrier_semaphore()
-
-    def others(action):
-        def one(other):
-            other = jnp.where(other == N_DEV - 1, 0, other + 1)
-            action(other)
-            return other
-
-        other = me
-        for _ in range(7):
-            other = one(other)
-
-        def eight(i, other):
-            for _ in range(8):
-                other = one(other)
-            return other
-
-        lax.fori_loop(1, N_DEV // 8, eight, other)
-
-    others(
-        lambda other: pl.semaphore_signal(
-            barrier, inc=1, device_id=other, device_id_type=LOGICAL
-        )
-    )
     for c in loads:
         c.wait()
 
@@ -244,20 +247,33 @@
 
     lax.fori_loop(0, 18, lift_pair, 0, unroll=LIFT_UNROLL)
 
-    def conv_pair(m, carry):
+    def conv_of(m):
         at = pl.multiple_of((2 * m + 1) * 192, 64)
-        act = mm(wconv[...], l3[pl.ds(at, 768), :])
-        sig = 0.5 * jnp.tanh(0.5 * act) + 0.5
-        hidden = (act * sig).astype(BF16)
+        return mm(wconv[...], l3[pl.ds(at, 768), :])
+
+    def activate(m, act):
         to = pl.multiple_of(m * 128, 128)
-        hid[pl.ds(to, 128), :] = hidden
-        dsl[pl.ds(to, 128), :] = sig * (1.0 + act * (1.0 - sig))
         row = pl.multiple_of(m * 16, 16)
         prow = pl.multiple_of(m * 16 + 16, 16)
-        fore[pl.ds(row, 16), :] = p3[1, pl.ds(prow, 16), :].astype(F32) + mm(bd_read_t, hidden)
+        sig = 0.5 * jnp.tanh(0.5 * act) + 0.5
+        value = act * sig
+        hidden = value.astype(BF16)
+        slope = sig + value * (1.0 - sig)
+        increment = mm(bd_read_t, hidden)
+        hid[pl.ds(to, 128), :] = hidden
+        dsl[pl.ds(to, 128), :] = slope
+        fore[pl.ds(row, 16), :] = p3[1, pl.ds(prow, 16), :].astype(F32) + increment
+
+    def conv_pair(m, carry):
+        before = acts[lax.rem(m + 1, 2)]
+        act = conv_of(m)
+        activate(m - 1, before)
+        acts[lax.rem(m, 2)] = act
         return carry
 
-    lax.fori_loop(0, 16, conv_pair, 0, unroll=CONV_UNROLL)
+    acts[0] = conv_of(0)
+    lax.fori_loop(1, 16, conv_pair, 0, unroll=CONV_UNROLL)
+    activate(15, acts[1])
     perm_t = onehot((r // 32 == c % 8) & (r % 32 == c // 8))
     est_ref[...] = mm(perm_t, fore[...].astype(BF16)).astype(BF16).reshape(8, 32, 256)
 
@@ -321,30 +337,36 @@
         )
     mine = jnp.concatenate(parts, axis=0)
     tbuf[...] = mine
-    arr1[pl.ds(lon, 1)] = mine[None]
-    for i in range(1, N_LON):
+    group = x * 2 + core
+    spot = y * 4 + z
+    home = y * 32 + z * 4
+    place_xc = at_xc(x, core)
+    arr1[pl.ds(group, 1)] = mine[None]
+    for k in (4, 5, 2, 3, 6, 7, 1):
+        other = lax.rem(group + k, 8)
         pltpu.make_async_remote_copy(
-            tbuf, arr1.at[lon], ar_ss.at[0], ar1_rs,
-            device_id=(face, lax.rem(lon + i, N_LON)), device_id_type=MESH,
+            tbuf, arr1.at[group], ar_ss.at[0], ar1_rs,
+            device_id=home + at_xc(other // 2, other % 2), device_id_type=LOGICAL,
         ).start()
-    pltpu.make_async_copy(
-        arr1.at[pl.ds(0, N_LON - 1)], arr1.at[pl.ds(0, N_LON - 1)], ar1_rs
-    ).wait()
+    pltpu.make_async_copy(arr1.at[pl.ds(0, 7)], arr1.at[pl.ds(0, 7)], ar1_rs).wait()
     total = arr1[0]
-    for k in range(1, N_LON):
+    for k in range(1, 8):
         total = total + arr1[k]
     sum1[...] = total
-    arr2[pl.ds(face, 1)] = total[None]
-    for i in range(1, N_FACE):
+    arr2[pl.ds(spot, 1)] = total[None]
+    ring = sorted(
+        ((dy, dz) for dy in range(4) for dz in range(4)),
+        key=lambda d: -(min(d[0], 4 - d[0]) + min(d[1], 4 - d[1])),
+    )
+    for dy, dz in ring[:-1]:
         pltpu.make_async_remote_copy(
-            sum1, arr2.at[face], ar_ss.at[1], ar2_rs,
-            device_id=(lax.rem(face + i, N_FACE), lon), device_id_type=MESH,
+            sum1, arr2.at[spot], ar_ss.at[1], ar2_rs,
+            device_id=lax.rem(y + dy, 4) * 32 + lax.rem(z + dz, 4) * 4 + place_xc,
+            device_id_type=LOGICAL,
         ).start()
-    pltpu.make_async_copy(
-        arr2.at[pl.ds(0, N_FACE - 1)], arr2.at[pl.ds(0, N_FACE - 1)], ar2_rs
-    ).wait()
+    pltpu.make_async_copy(arr2.at[pl.ds(0, 15)], arr2.at[pl.ds(0, 15)], ar2_rs).wait()
     total = arr2[0]
-    for k in range(1, N_FACE):
+    for k in range(1, 16):
         total = total + arr2[k]
     tot_ref[...] = total
 
@@ -355,10 +377,10 @@
         send.at[pl.ds(0, N_DEV - 1)], send.at[pl.ds(0, N_DEV - 1)], pay_ss
     ).wait()
     pltpu.make_async_copy(
-        arr1.at[pl.ds(0, N_LON - 1)], arr1.at[pl.ds(0, N_LON - 1)], ar_ss.at[0]
+        arr1.at[pl.ds(0, 7)], arr1.at[pl.ds(0, 7)], ar_ss.at[0]
     ).wait()
     pltpu.make_async_copy(
-        arr2.at[pl.ds(0, N_FACE - 1)], arr2.at[pl.ds(0, N_FACE - 1)], ar_ss.at[1]
+        arr2.at[pl.ds(0, 15)], arr2.at[pl.ds(0, 15)], ar_ss.at[1]
     ).wait()
 
 
@@ -430,7 +452,7 @@
             V((16, 256), BF16), V((16, 256), BF16), V((6, 16, 256), BF16), V((2, 16, 256), BF16),
             V((3, 288, 256), BF16), V((36 * 192, 256), BF16), V((128, 768), BF16),
             V((256, 256), F32), V((256, 256), BF16), V((2048, 256), BF16), V((2048, 256), F32),
-            V((16, 40, 128), F32), V((8, 40, 128), F32), V((40, 128), F32), V((40, 128), F32),
+            V((2, 128, 256), F32), V((8, 40, 128), F32), V((16, 40, 128), F32), V((40, 128), F32), V((40, 128), F32),
             DMA((7,)), DMA((WEIGHT_CHUNKS,)), DMA, DMA, DMA, DMA, DMA,
             DMA((8,)), DMA((8,)), DMA((2,)), DMA, DMA,
         ],

time: 39.1 us -> 35.9 us (0.918)
  Pallas kernels: 38.3 us -> 35.1 us
    pallas_call x1, Pallas kernels: 36.9 us -> 33.6 us  [per_device(): pl.pallas_call(step_kernel, out_shape=(jax.ShapeDtypeStruct((8, 32, 256),...]
where the time goes in v2:
time: 35.9 us; the launch traced here: 35.8 us
  Pallas kernels  35.1 us (98%)
  between operations  0.67 us (2%)
    pallas_call x1, Pallas kernels, per_device(): pl.pallas_call(step_kernel, out_shape=(jax.ShapeDtypeStruct((8, 32, 256),...  33.6 us
    pallas_call x1, Pallas kernels, per_device(): pl.pallas_call(final_kernel, out_shape=(jax.ShapeDtypeStruct((8, 32, 256)...  1.47 us

profile of v2, /device:TPU:1, one launch (start us, length us, event | category | flops | bytes accessed | tf_op | source)
XLA Modules:
  0.0 35.8 jit_solution(11703666849948516818)
XLA Ops:
  0.6 0.0 copy-start
  0.6 0.0 copy-start.1
  0.7 33.6 %step.1 = (bf16[8,32,256]{2,1,0:T(8,128)(2,1)S(1)}, bf16[8,32,256]{2,1,0:T(8,128)(2,1)S(1)}, f32[40,128]{1,0:T(8,128)S(1)}) custom-call(bf16[32,8,128]{2,1,0:T(8,128)(2,1)} %src_hbm.1, bf16[32,4,128,128]{3,2,1,0:T(8,128)(2,1)} %wts_hbm.1, s32[4,32]{1,0:T(4,128)} %bitcast.4, s32[4,32]{1,0:T(4,128)} %bitcast.5, bf16[8,32,256]{2,1,0:T(8,128)(2,1)} %prior_hbm.1, ...), custom_call_target="tpu_custom_call" | custom-call | tf_op jit(solution)/shard_map/step/pallas_call | solution.py:437
  34.3 0.0 copy-done
  34.3 0.0 copy-done.1
  34.3 1.5 %final.1 = (bf16[8,32,256]{2,1,0:T(8,128)(2,1)}, bf16[8,32,256]{2,1,0:T(8,128)(2,1)}, f32[8,64]{1,0:T(8,128)}, f32[9,64,64]{2,1,0:T(8,128)}, f32[8,64]{1,0:T(8,128)}) custom-call(f32[40,128]{1,0:T(8,128)S(1)} %get-tuple-element.13.tot_any, bf16[8,32,256]{2,1,0:T(8,128)(2,1)S(1)} %get-tuple-element.14.rem_any, ...), custom_call_target="tpu_custom_call" | custom-call | tf_op jit(solution)/shard_map/final/pallas_call | solution.py:467
Async XLA Ops:
  0.6 33.7 %copy-start = (bf16[9,64,64]{2,1,0:T(8,128)(2,1)S(1)}, bf16[9,64,64]{2,1,0:T(8,128)(2,1)}, u32[]{:S(2)}) copy-start(bf16[9,64,64]{2,1,0:T(8,128)(2,1)} %kern.1) | copy-start | bytes 221188
  0.6 33.7 %copy-start.1 = (bf16[8,64]{1,0:T(8,128)(2,1)S(1)}, bf16[8,64]{1,0:T(8,128)(2,1)}, u32[]{:S(2)}) copy-start(bf16[8,64]{1,0:T(8,128)(2,1)} %lift.1) | copy-start | bytes 3076

commit v3 on v2

--- a/solution.py
+++ b/solution.py
@@ -11,7 +11,7 @@
 N_DEV = N_FACE * N_LON
 NT = (((1,), (1,)), ((), ()))
 WEIGHT_CHUNKS = 4
-LIFT_UNROLL, CONV_UNROLL, GRAD_UNROLL = 3, 3, 8
+CONV_UNROLL, GRAD_UNROLL = 16, 16
 
 
 def mm(a, b):
@@ -33,12 +33,21 @@
     return jnp.where(mask, 1.0, 0.0).astype(BF16)
 
 
+FAR_FIRST = sorted(
+    [
+        (dy, dx, dz, dc)
+        for dy in range(4) for dx in range(4) for dz in range(4) for dc in range(2)
+    ][1:],
+    key=lambda d: -sum(min(v, 4 - v) for v in d[:3]),
+)
+
+
 def step_kernel(
     src_hbm, wts_hbm, tile_hbm, row_hbm, prior_hbm, lift_hbm, kern_hbm, read_hbm,
     rem_ref, est_ref, tot_ref,
     src, wts, dtile, drow, prior, lift, kern, read,
-    contrib, idx_v, idx_s, lab_out, lab_in, send, recv, wide,
-    er_out, ec_out, er_in, ec_in, p3, l3, wconv, fore, mis_ref, hid, dsl, acts, arr1, arr2, sum1,
+    contrib, idx_v, idx_s, lab1_out, lab1_in, lab2_out, lab2_in, send, recv, wide,
+    er_out, ec_out, er_in, ec_in, p3, l3, wconv, fore, mis_ref, hid, dsl, edges, arr1, arr2, sum1,
     tbuf,
     in_sem, w_sem, idx_sem, lab_ss, lab_rs, pay_ss, pay_rs,
     halo_ss, halo_rs, ar_ss, ar1_rs, ar2_rs,
@@ -49,25 +58,22 @@
     y, z = face // 2, lon // 4
     x = (face % 2) * 2 + (lon // 2) % 2
     core = lon % 2
+    group, spot = x * 2 + core, y * 4 + z
+    home = y * 32 + z * 4
+    here = spot * 8 + group
 
     def at_xc(x_at, core_at):
         return (x_at // 2) * 16 + (x_at % 2) * 2 + core_at
 
     barrier = pltpu.get_barrier_semaphore()
 
+    y_at = [lax.rem(y + d, 4) * 32 for d in range(4)]
+    x_at = [at_xc(lax.rem(x + d, 4), 0) for d in range(4)]
+    zc_at = [lax.rem(z + d // 2, 4) * 4 + lax.rem(core + d % 2, 2) for d in range(8)]
+
     def others(action):
-        zc = []
-        for dz, dc in ((2, 1), (2, 0), (1, 1), (3, 1), (1, 0), (3, 0), (0, 1), (0, 0)):
-            zc.append((lax.rem(z + dz, 4) * 4 + lax.rem(core + dc, 2), (dz, dc)))
-        far = sorted(
-            ((dy, dx) for dy in range(4) for dx in range(4)),
-            key=lambda d: -(min(d[0], 4 - d[0]) + min(d[1], 4 - d[1])),
-        )
-        for dy, dx in far:
-            base = lax.rem(y + dy, 4) * 32 + at_xc(lax.rem(x + dx, 4), 0)
-            for offset, d in zc:
-                if (dy, dx) + d != (0, 0, 0, 0):
-                    action(base + offset)
+        for dy, dx, dz, dc in FAR_FIRST:
+            action(y_at[dy] + x_at[dx] + zc_at[2 * dz + dc])
 
     others(
         lambda other: pl.semaphore_signal(
@@ -112,10 +118,12 @@
     idx_copy = pltpu.make_async_copy(idx_v, idx_s, idx_sem)
     idx_copy.start()
     l_col = jnp.broadcast_to(l_row, (128, 128)).T
-    labels = jnp.where(pos - 2 * d_col == ci % 2, l_col + 1, 0).astype(F32).astype(BF16)
-    code = (mm(onehot(d_mat == ri), labels) - 1.0).astype(I32)
-    lab_out[...] = code.reshape(128, 1, 128)
-    lab_in[pl.ds(me, 1)] = lab_out[pl.ds(me, 1)]
+    spots = (d_col // 32) * 4 + (d_col // 4) % 4
+    labels = jnp.where(spots * 2 + pos - 2 * d_col == ci, l_col + 1, 0).astype(F32).astype(BF16)
+    d_few = d_mat[0:16]
+    owners = onehot(((d_few // 16) % 2) * 4 + d_few % 4 == ri[0:16])
+    lab1_out[...] = mm(owners, labels)[0:8].astype(I32).reshape(8, 1, 128)
+    lab1_in[pl.ds(group, 1)] = lab1_out[pl.ds(group, 1)]
 
     r, c = rc(256, 256)
     perm = onehot((r // 8 == c % 32) & (r % 8 == c // 32))
@@ -129,6 +137,57 @@
     r16, c16 = rc(16, 256)
     edge = onehot(((r16 == 0) & (c16 == 0)) | ((r16 == 1) & (c16 == 255)))
     ec_out[...] = nt(edge, pb).astype(BF16)
+
+    for chunk in range(WEIGHT_CHUNKS):
+        wloads[chunk].wait()
+
+        def regrid(s, carry):
+            block = jnp.concatenate([wts[s, k] for k in range(4)], axis=1)
+            out = mm(src[s], block)
+            for k in range(4):
+                contrib[k * 32 + s] = out[:, k * 128 : (k + 1) * 128].astype(BF16).astype(F32)
+            return carry
+
+        lax.fori_loop(chunk * per, (chunk + 1) * per, regrid, 0, unroll=per)
+    idx_copy.wait()
+
+    def place(d, carry):
+        a = contrib[idx_s[0, 2 * d]]
+        b = contrib[idx_s[0, 2 * d + 1]]
+        send[d] = jnp.concatenate([a, b], axis=0).astype(BF16)
+        return carry
+
+    lax.fori_loop(0, N_DEV, place, 0, unroll=16)
+    recv[pl.ds(here, 1)] = send[pl.ds(me, 1)]
+
+    pl.semaphore_wait(barrier, N_DEV - 1)
+
+    up, down = lax.rem(face + N_FACE - 1, N_FACE), lax.rem(face + 1, N_FACE)
+    left, right = lax.rem(lon + N_LON - 1, N_LON), lax.rem(lon + 1, N_LON)
+    halos = []
+    ways = [(up, left), (up, lon), (up, right), (down, left), (down, lon), (down, right)]
+    for k, (f, l) in enumerate(ways):
+        halos.append(
+            pltpu.make_async_remote_copy(
+                er_out, er_in.at[5 - k], halo_ss.at[k], halo_rs.at[5 - k],
+                device_id=(f, l), device_id_type=MESH,
+            )
+        )
+    for k, l in enumerate((left, right)):
+        halos.append(
+            pltpu.make_async_remote_copy(
+                ec_out, ec_in.at[1 - k], halo_ss.at[6 + k], halo_rs.at[7 - k],
+                device_id=(face, l), device_id_type=MESH,
+            )
+        )
+    for h in halos:
+        h.start()
+    for k in (4, 5, 2, 3, 6, 7, 1):
+        other = lax.rem(group + k, 8)
+        pltpu.make_async_remote_copy(
+            lab1_out.at[other], lab1_in.at[group], lab_ss.at[0], lab_rs.at[0],
+            device_id=home + at_xc(other // 2, other % 2), device_id_type=LOGICAL,
+        ).start()
 
     i64r, i64c = rc(128, 64)
     eye2 = onehot(i64r % 64 == i64c)
@@ -152,62 +211,53 @@
     wconv[0:64, :] = nt(eye1, jnp.concatenate([taps, zeros], axis=0)).astype(BF16)
     wconv[64:128, :] = nt(eye1, jnp.concatenate([zeros, taps], axis=0)).astype(BF16)
 
-    for chunk in range(WEIGHT_CHUNKS):
-        wloads[chunk].wait()
-
-        def regrid(s, carry):
-            block = jnp.concatenate([wts[s, k] for k in range(4)], axis=1)
-            out = mm(src[s], block)
-            for k in range(4):
-                contrib[k * 32 + s] = out[:, k * 128 : (k + 1) * 128].astype(BF16).astype(F32)
-            return carry
-
-        lax.fori_loop(chunk * per, (chunk + 1) * per, regrid, 0, unroll=4)
-    idx_copy.wait()
-
-    def place(d, carry):
-        a = contrib[idx_s[0, 2 * d]]
-        b = contrib[idx_s[0, 2 * d + 1]]
-        send[d] = jnp.concatenate([a, b], axis=0).astype(BF16)
+    p3[0, pl.ds(16, 256), :] = mm(pb, shift0).astype(BF16)
+    p3[2, pl.ds(16, 256), :] = mm(pb, shift2).astype(BF16)
+
+    def lift_pair(m, carry):
+        at = pl.multiple_of(m * 16, 16)
+        for j in range(3):
+            out = mm(bd_lift, p3[j, pl.ds(at, 16), :]).astype(BF16)
+            for e in range(2):
+                to = pl.multiple_of((2 * m + e) * 192 + j * 64, 64)
+                l3[pl.ds(to, 64), :] = out[e * 64 : (e + 1) * 64]
         return carry
-
-    lax.fori_loop(0, N_DEV, place, 0, unroll=16)
-    recv[pl.ds(me, 1)] = send[pl.ds(me, 1)]
-
-    pl.semaphore_wait(barrier, N_DEV - 1)
-
-    up, down = lax.rem(face + N_FACE - 1, N_FACE), lax.rem(face + 1, N_FACE)
-    left, right = lax.rem(lon + N_LON - 1, N_LON), lax.rem(lon + 1, N_LON)
-    halos = []
-    ways = [(up, left), (up, lon), (up, right), (down, left), (down, lon), (down, right)]
-    for k, (f, l) in enumerate(ways):
-        halos.append(
-            pltpu.make_async_remote_copy(
-                er_out, er_in.at[5 - k], halo_ss.at[k], halo_rs.at[5 - k],
-                device_id=(f, l), device_id_type=MESH,
-            )
-        )
-    for k, l in enumerate((left, right)):
-        halos.append(
-            pltpu.make_async_remote_copy(
-                ec_out, ec_in.at[1 - k], halo_ss.at[6 + k], halo_rs.at[7 - k],
-                device_id=(face, l), device_id_type=MESH,
-            )
-        )
-    for h in halos:
-        h.start()
 
     def send_block(other):
         pltpu.make_async_remote_copy(
-            send.at[other], recv.at[me], pay_ss, pay_rs,
+            send.at[other], recv.at[here], pay_ss, pay_rs,
             device_id=other, device_id_type=LOGICAL,
         ).start()
+
+    others(send_block)
+    for m in range(1, 17):
+        lift_pair(m, 0)
+
+    pltpu.make_async_copy(lab1_in.at[pl.ds(0, 7)], lab1_in.at[pl.ds(0, 7)], lab_rs.at[0]).wait()
+    came = lab1_in[...].reshape(8, 128).astype(F32).astype(BF16)
+    vr, vc = rc(128, 8)
+    spread = mm(onehot((vr % 16) // 2 == vc), came)
+    spread = jnp.where(ri % 2 == ci % 2, spread, 0.0).astype(BF16)
+    lab2_out[...] = (
+        nt(onehot(ri[0:16] == ci[0:16] // 2), spread).astype(I32).reshape(16, 1, 128)
+    )
+    lab2_in[pl.ds(spot, 1)] = lab2_out[pl.ds(spot, 1)]
+    place_xc = at_xc(x, core)
+    ring = sorted(
+        ((dy, dz) for dy in range(4) for dz in range(4)),
+        key=lambda d: -(min(d[0], 4 - d[0]) + min(d[1], 4 - d[1])),
+    )[:-1]
+
+    def in_ring(dy, dz):
+        there_y, there_z = lax.rem(y + dy, 4), lax.rem(z + dz, 4)
+        return there_y * 4 + there_z, there_y * 32 + there_z * 4 + place_xc
+
+    for dy, dz in ring:
+        other, device = in_ring(dy, dz)
         pltpu.make_async_remote_copy(
-            lab_out.at[other], lab_in.at[me], lab_ss, lab_rs,
-            device_id=other, device_id_type=LOGICAL,
+            lab2_out.at[other], lab2_in.at[spot], lab_ss.at[1], lab_rs.at[1],
+            device_id=device, device_id_type=LOGICAL,
         ).start()
-
-    others(send_block)
 
     for h in halos:
         h.wait()
@@ -228,24 +278,30 @@
     for j, outer in ((0, outer0), (1, mid), (2, outer2)):
         p3[j, pl.ds(0, 16), :] = outer[0:16]
         p3[j, pl.ds(272, 16), :] = outer[16:32]
-    col0 = onehot((r16 == 1) & (c16 == 0))
-    col2 = onehot((r16 == 0) & (c16 == 255))
-    pb = p3[1, pl.ds(16, 256), :]
-    from_left = nt(eye, ec_in[0]).astype(BF16)
-    from_right = nt(eye, ec_in[1]).astype(BF16)
-    p3[0, pl.ds(16, 256), :] = (mm(pb, shift0) + mm(from_left, col0)).astype(BF16)
-    p3[2, pl.ds(16, 256), :] = (mm(pb, shift2) + mm(from_right, col2)).astype(BF16)
-
-    def lift_pair(m, carry):
+    halo_cols = []
+    for e, (keep, src_row, lane) in enumerate(((ec_in[0], 1, 0), (ec_in[1], 0, 127))):
+        sel = onehot((c16[:, 0:128] == lane) & (r16[:, 0:128] == src_row))
+        halo_cols.append(mm(nt(eye, keep).astype(BF16), sel).astype(BF16))
+        p3[2 * e, pl.ds(16, 256), pl.ds(128 * e, 128)] = (
+            p3[2 * e, pl.ds(16, 256), pl.ds(128 * e, 128)] + halo_cols[e]
+        )
+        edges[e] = halo_cols[e]
+
+    for m in (0, 17):
+        lift_pair(m, 0)
+
+    def lift_edges(m, carry):
         at = pl.multiple_of(m * 16, 16)
-        for j in range(3):
-            out = mm(bd_lift, p3[j, pl.ds(at, 16), :]).astype(BF16)
-            for e in range(2):
-                to = pl.multiple_of((2 * m + e) * 192 + j * 64, 64)
-                l3[pl.ds(to, 64), :] = out[e * 64 : (e + 1) * 64]
+        for e in range(2):
+            out = mm(bd_lift, edges[e, pl.ds(at, 16), :]).astype(BF16)
+            for k in range(2):
+                to = pl.multiple_of((2 * m + 2 + k) * 192 + 128 * e, 64)
+                l3[pl.ds(to, 64), pl.ds(128 * e, 128)] = (
+                    l3[pl.ds(to, 64), pl.ds(128 * e, 128)] + out[k * 64 : (k + 1) * 64]
+                )
         return carry
 
-    lax.fori_loop(0, 18, lift_pair, 0, unroll=LIFT_UNROLL)
+    lax.fori_loop(0, 16, lift_edges, 0, unroll=4)
 
     def conv_of(m):
         at = pl.multiple_of((2 * m + 1) * 192, 64)
@@ -253,45 +309,36 @@
 
     def activate(m, act):
         to = pl.multiple_of(m * 128, 128)
+        sig = 0.5 * jnp.tanh(0.5 * act) + 0.5
+        value = act * sig
+        hid[pl.ds(to, 128), :] = value.astype(BF16)
+        dsl[pl.ds(to, 128), :] = sig + value * (1.0 - sig)
+
+    def conv_pair(m, carry):
+        activate(m, conv_of(m))
+        return carry
+
+    lax.fori_loop(0, 16, conv_pair, 0, unroll=CONV_UNROLL)
+
+    def read_pair(m, carry):
+        to = pl.multiple_of(m * 128, 128)
         row = pl.multiple_of(m * 16, 16)
         prow = pl.multiple_of(m * 16 + 16, 16)
-        sig = 0.5 * jnp.tanh(0.5 * act) + 0.5
-        value = act * sig
-        hidden = value.astype(BF16)
-        slope = sig + value * (1.0 - sig)
-        increment = mm(bd_read_t, hidden)
-        hid[pl.ds(to, 128), :] = hidden
-        dsl[pl.ds(to, 128), :] = slope
-        fore[pl.ds(row, 16), :] = p3[1, pl.ds(prow, 16), :].astype(F32) + increment
-
-    def conv_pair(m, carry):
-        before = acts[lax.rem(m + 1, 2)]
-        act = conv_of(m)
-        activate(m - 1, before)
-        acts[lax.rem(m, 2)] = act
+        fore[pl.ds(row, 16), :] = p3[1, pl.ds(prow, 16), :].astype(F32) + mm(
+            bd_read_t, hid[pl.ds(to, 128), :]
+        )
         return carry
 
-    acts[0] = conv_of(0)
-    lax.fori_loop(1, 16, conv_pair, 0, unroll=CONV_UNROLL)
-    activate(15, acts[1])
+    lax.fori_loop(0, 16, read_pair, 0, unroll=4)
     perm_t = onehot((r // 32 == c % 8) & (r % 32 == c // 8))
     est_ref[...] = mm(perm_t, fore[...].astype(BF16)).astype(BF16).reshape(8, 32, 256)
 
-    pltpu.make_async_copy(
-        lab_in.at[pl.ds(0, N_DEV - 1)], lab_in.at[pl.ds(0, N_DEV - 1)], lab_rs
-    ).wait()
-    lab = lab_in[...].reshape(128, 128)
-    lr, lc = rc(64, 128)
-    mine_mask = lr == lc // 2
-    lane_label = jnp.concatenate(
-        [
-            jnp.sum(jnp.where(mine_mask, lab[at : at + 64], 0), axis=0, keepdims=True)
-            for at in (0, 64)
-        ],
-        axis=1,
-    )
+    pltpu.make_async_copy(lab2_in.at[pl.ds(0, 15)], lab2_in.at[pl.ds(0, 15)], lab_rs.at[1]).wait()
+    lab = lab2_in[...].reshape(16, 128)
+    lab = jnp.concatenate([lab, lab], axis=1)
+    lane_label = jnp.sum(jnp.where(c16 // 16 == r16, lab, 0), axis=0, keepdims=True)
     hr, _ = rc(64, 256)
-    picker = onehot(jnp.broadcast_to(lane_label, (64, 256)) == 2 * (hr % 32) + hr // 32)
+    picker = onehot(jnp.broadcast_to(lane_label, (64, 256)) == 2 * (hr % 32) + hr // 32 + 1)
     pltpu.make_async_copy(
         recv.at[pl.ds(0, N_DEV - 1)], recv.at[pl.ds(0, N_DEV - 1)], pay_rs
     ).wait()
@@ -337,10 +384,6 @@
         )
     mine = jnp.concatenate(parts, axis=0)
     tbuf[...] = mine
-    group = x * 2 + core
-    spot = y * 4 + z
-    home = y * 32 + z * 4
-    place_xc = at_xc(x, core)
     arr1[pl.ds(group, 1)] = mine[None]
     for k in (4, 5, 2, 3, 6, 7, 1):
         other = lax.rem(group + k, 8)
@@ -354,15 +397,10 @@
         total = total + arr1[k]
     sum1[...] = total
     arr2[pl.ds(spot, 1)] = total[None]
-    ring = sorted(
-        ((dy, dz) for dy in range(4) for dz in range(4)),
-        key=lambda d: -(min(d[0], 4 - d[0]) + min(d[1], 4 - d[1])),
-    )
-    for dy, dz in ring[:-1]:
+    for dy, dz in ring:
         pltpu.make_async_remote_copy(
             sum1, arr2.at[spot], ar_ss.at[1], ar2_rs,
-            device_id=lax.rem(y + dy, 4) * 32 + lax.rem(z + dz, 4) * 4 + place_xc,
-            device_id_type=LOGICAL,
+            device_id=in_ring(dy, dz)[1], device_id_type=LOGICAL,
         ).start()
     pltpu.make_async_copy(arr2.at[pl.ds(0, 15)], arr2.at[pl.ds(0, 15)], ar2_rs).wait()
     total = arr2[0]
@@ -370,9 +408,8 @@
         total = total + arr2[k]
     tot_ref[...] = total
 
-    pltpu.make_async_copy(
-        lab_out.at[pl.ds(0, N_DEV - 1)], lab_out.at[pl.ds(0, N_DEV - 1)], lab_ss
-    ).wait()
+    pltpu.make_async_copy(lab1_in.at[pl.ds(0, 7)], lab1_in.at[pl.ds(0, 7)], lab_ss.at[0]).wait()
+    pltpu.make_async_copy(lab2_in.at[pl.ds(0, 15)], lab2_in.at[pl.ds(0, 15)], lab_ss.at[1]).wait()
     pltpu.make_async_copy(
         send.at[pl.ds(0, N_DEV - 1)], send.at[pl.ds(0, N_DEV - 1)], pay_ss
     ).wait()
@@ -447,13 +484,13 @@
             V((32, 8, 128), BF16), V((32, 4, 128, 128), BF16), V((4, 32), I32), V((4, 32), I32),
             V((8, 32, 256), BF16), V((8, 64), BF16), V((9, 64, 64), BF16), V((8, 64), BF16),
             V((128, 8, 128), F32), V((1, 256), I32), pltpu.SMEM((1, 256), I32),
-            V((128, 1, 128), I32), V((128, 1, 128), I32),
+            V((8, 1, 128), I32), V((8, 1, 128), I32), V((16, 1, 128), I32), V((16, 1, 128), I32),
             V((128, 16, 128), BF16), V((128, 16, 128), BF16), V((2048, 128), F32),
             V((16, 256), BF16), V((16, 256), BF16), V((6, 16, 256), BF16), V((2, 16, 256), BF16),
             V((3, 288, 256), BF16), V((36 * 192, 256), BF16), V((128, 768), BF16),
             V((256, 256), F32), V((256, 256), BF16), V((2048, 256), BF16), V((2048, 256), F32),
-            V((2, 128, 256), F32), V((8, 40, 128), F32), V((16, 40, 128), F32), V((40, 128), F32), V((40, 128), F32),
-            DMA((7,)), DMA((WEIGHT_CHUNKS,)), DMA, DMA, DMA, DMA, DMA,
+            V((2, 256, 128), BF16), V((8, 40, 128), F32), V((16, 40, 128), F32), V((40, 128), F32), V((40, 128), F32),
+            DMA((7,)), DMA((WEIGHT_CHUNKS,)), DMA, DMA((2,)), DMA((2,)), DMA, DMA,
             DMA((8,)), DMA((8,)), DMA((2,)), DMA, DMA,
         ],
         compiler_params=pltpu.CompilerParams(

time: 35.9 us -> 34.4 us (0.958)
  Pallas kernels: 35.1 us -> 33.6 us
    pallas_call x1, Pallas kernels: 33.6 us -> 32.1 us  [per_device(): pl.pallas_call(step_kernel, out_shape=(jax.ShapeDtypeStruct((8, 32, 256),...]
where the time goes in v3:
time: 34.4 us; the launch traced here: 34.3 us
  Pallas kernels  33.6 us (98%)
  between operations  0.67 us (2%)
    pallas_call x1, Pallas kernels, per_device(): pl.pallas_call(step_kernel, out_shape=(jax.ShapeDtypeStruct((8, 32, 256),...  32.1 us
    pallas_call x1, Pallas kernels, per_device(): pl.pallas_call(final_kernel, out_shape=(jax.ShapeDtypeStruct((8, 32, 256)...  1.47 us

profile of v3, /device:TPU:1, one launch (start us, length us, event | category | flops | bytes accessed | tf_op | source)
XLA Modules:
  0.0 34.3 jit_solution(3578734646355270090)
XLA Ops:
  0.6 0.0 copy-start
  0.6 0.0 copy-start.1
  0.7 32.1 %step.1 = (bf16[8,32,256]{2,1,0:T(8,128)(2,1)S(1)}, bf16[8,32,256]{2,1,0:T(8,128)(2,1)S(1)}, f32[40,128]{1,0:T(8,128)S(1)}) custom-call(bf16[32,8,128]{2,1,0:T(8,128)(2,1)} %src_hbm.1, bf16[32,4,128,128]{3,2,1,0:T(8,128)(2,1)} %wts_hbm.1, s32[4,32]{1,0:T(4,128)} %bitcast.4, s32[4,32]{1,0:T(4,128)} %bitcast.5, bf16[8,32,256]{2,1,0:T(8,128)(2,1)} %prior_hbm.1, ...), custom_call_target="tpu_custom_call" | custom-call | tf_op jit(solution)/shard_map/step/pallas_call | solution.py:474
  32.8 0.0 copy-done
  32.8 0.0 copy-done.1
  32.8 1.5 %final.1 = (bf16[8,32,256]{2,1,0:T(8,128)(2,1)}, bf16[8,32,256]{2,1,0:T(8,128)(2,1)}, f32[8,64]{1,0:T(8,128)}, f32[9,64,64]{2,1,0:T(8,128)}, f32[8,64]{1,0:T(8,128)}) custom-call(f32[40,128]{1,0:T(8,128)S(1)} %get-tuple-element.13.tot_any, bf16[8,32,256]{2,1,0:T(8,128)(2,1)S(1)} %get-tuple-element.14.rem_any, ...), custom_call_target="tpu_custom_call" | custom-call | tf_op jit(solution)/shard_map/final/pallas_call | solution.py:504
Async XLA Ops:
  0.6 32.2 %copy-start = (bf16[9,64,64]{2,1,0:T(8,128)(2,1)S(1)}, bf16[9,64,64]{2,1,0:T(8,128)(2,1)}, u32[]{:S(2)}) copy-start(bf16[9,64,64]{2,1,0:T(8,128)(2,1)} %kern.1) | copy-start | bytes 221188
  0.6 32.2 %copy-start.1 = (bf16[8,64]{1,0:T(8,128)(2,1)S(1)}, bf16[8,64]{1,0:T(8,128)(2,1)}, u32[]{:S(2)}) copy-start(bf16[8,64]{1,0:T(8,128)(2,1)} %lift.1) | copy-start | bytes 3076

commit v4 on v3

--- a/solution.py
+++ b/solution.py
@@ -71,15 +71,14 @@
     x_at = [at_xc(lax.rem(x + d, 4), 0) for d in range(4)]
     zc_at = [lax.rem(z + d // 2, 4) * 4 + lax.rem(core + d % 2, 2) for d in range(8)]
 
-    def others(action):
-        for dy, dx, dz, dc in FAR_FIRST:
+    def others(action, order=FAR_FIRST):
+        for dy, dx, dz, dc in order:
             action(y_at[dy] + x_at[dx] + zc_at[2 * dz + dc])
 
-    others(
-        lambda other: pl.semaphore_signal(
-            barrier, inc=1, device_id=other, device_id_type=LOGICAL
-        )
-    )
+    def greet(other):
+        pl.semaphore_signal(barrier, inc=1, device_id=other, device_id_type=LOGICAL)
+
+    others(greet, FAR_FIRST[:40])
     small = [
         (tile_hbm, dtile), (row_hbm, drow), (prior_hbm, prior), (src_hbm, src),
         (lift_hbm, lift), (kern_hbm, kern), (read_hbm, read),
@@ -97,6 +96,7 @@
     for c in wloads:
         c.start()
 
+    others(greet, FAR_FIRST[40:])
     for c in loads:
         c.wait()
 
@@ -278,30 +278,26 @@
     for j, outer in ((0, outer0), (1, mid), (2, outer2)):
         p3[j, pl.ds(0, 16), :] = outer[0:16]
         p3[j, pl.ds(272, 16), :] = outer[16:32]
-    halo_cols = []
-    for e, (keep, src_row, lane) in enumerate(((ec_in[0], 1, 0), (ec_in[1], 0, 127))):
-        sel = onehot((c16[:, 0:128] == lane) & (r16[:, 0:128] == src_row))
-        halo_cols.append(mm(nt(eye, keep).astype(BF16), sel).astype(BF16))
-        p3[2 * e, pl.ds(16, 256), pl.ds(128 * e, 128)] = (
-            p3[2 * e, pl.ds(16, 256), pl.ds(128 * e, 128)] + halo_cols[e]
-        )
-        edges[e] = halo_cols[e]
+    for e, lane in ((0, 0), (1, 127)):
+        sel = onehot((c16[:, 0:128] == lane) & (r16[:, 0:128] == 1 - e))
+        column = mm(nt(eye, ec_in[e]).astype(BF16), sel).astype(BF16)
+        at = pl.ds(128 * e, 128)
+        p3[2 * e, pl.ds(16, 256), at] = p3[2 * e, pl.ds(16, 256), at] + column
+        edges[e] = column
+    edges[0] = edges[0] + edges[1]
 
     for m in (0, 17):
         lift_pair(m, 0)
 
-    def lift_edges(m, carry):
-        at = pl.multiple_of(m * 16, 16)
-        for e in range(2):
-            out = mm(bd_lift, edges[e, pl.ds(at, 16), :]).astype(BF16)
+    low_lanes = ci < 64
+    for m in range(16):
+        both = mm(bd_lift, edges[0, 16 * m : 16 * m + 16, :])
+        for e, keep in ((0, low_lanes), (1, jnp.logical_not(low_lanes))):
+            column = jnp.where(keep, both, 0.0).astype(BF16)
+            at = pl.ds(128 * e, 128)
             for k in range(2):
-                to = pl.multiple_of((2 * m + 2 + k) * 192 + 128 * e, 64)
-                l3[pl.ds(to, 64), pl.ds(128 * e, 128)] = (
-                    l3[pl.ds(to, 64), pl.ds(128 * e, 128)] + out[k * 64 : (k + 1) * 64]
-                )
-        return carry
-
-    lax.fori_loop(0, 16, lift_edges, 0, unroll=4)
+                to = pl.ds((2 * m + 2 + k) * 192 + 128 * e, 64)
+                l3[to, at] = l3[to, at] + column[k * 64 : (k + 1) * 64]
 
     def conv_of(m):
         at = pl.multiple_of((2 * m + 1) * 192, 64)
@@ -342,7 +338,7 @@
     pltpu.make_async_copy(
         recv.at[pl.ds(0, N_DEV - 1)], recv.at[pl.ds(0, N_DEV - 1)], pay_rs
     ).wait()
-    wide[...] = recv[...].reshape(2048, 128).astype(F32)
+    wide[pl.ds(0, 2048), :] = recv[...].reshape(2048, 128).astype(F32)
     fields = []
     for q in range(8):
         block = wide[pl.ds(q, 256, stride=8), :].astype(BF16)
@@ -485,7 +481,7 @@
             V((8, 32, 256), BF16), V((8, 64), BF16), V((9, 64, 64), BF16), V((8, 64), BF16),
             V((128, 8, 128), F32), V((1, 256), I32), pltpu.SMEM((1, 256), I32),
             V((8, 1, 128), I32), V((8, 1, 128), I32), V((16, 1, 128), I32), V((16, 1, 128), I32),
-            V((128, 16, 128), BF16), V((128, 16, 128), BF16), V((2048, 128), F32),
+            V((128, 16, 128), BF16), V((128, 16, 128), BF16), V((2056, 128), F32),
             V((16, 256), BF16), V((16, 256), BF16), V((6, 16, 256), BF16), V((2, 16, 256), BF16),
             V((3, 288, 256), BF16), V((36 * 192, 256), BF16), V((128, 768), BF16),
             V((256, 256), F32), V((256, 256), BF16), V((2048, 256), BF16), V((2048, 256), F32),

time: 34.4 us -> 34.6 us (level)
  no operation moved by 1% of the time
where the time goes in v4:
time: 34.6 us; the launch traced here: 34.4 us
  Pallas kernels  33.8 us (98%)
  between operations  0.67 us (2%)
    pallas_call x1, Pallas kernels, per_device(): pl.pallas_call(step_kernel, out_shape=(jax.ShapeDtypeStruct((8, 32, 256),...  32.3 us
    pallas_call x1, Pallas kernels, per_device(): pl.pallas_call(final_kernel, out_shape=(jax.ShapeDtypeStruct((8, 32, 256)...  1.47 us

profile of v4, /device:TPU:1, one launch (start us, length us, event | category | flops | bytes accessed | tf_op | source)
XLA Modules:
  0.0 34.4 jit_solution(951728368944387792)
XLA Ops:
  0.6 0.0 copy-start
  0.6 0.0 copy-start.1
  0.7 32.3 %step.1 = (bf16[8,32,256]{2,1,0:T(8,128)(2,1)S(1)}, bf16[8,32,256]{2,1,0:T(8,128)(2,1)S(1)}, f32[40,128]{1,0:T(8,128)S(1)}) custom-call(bf16[32,8,128]{2,1,0:T(8,128)(2,1)} %src_hbm.1, bf16[32,4,128,128]{3,2,1,0:T(8,128)(2,1)} %wts_hbm.1, s32[4,32]{1,0:T(4,128)} %bitcast.4, s32[4,32]{1,0:T(4,128)} %bitcast.5, bf16[8,32,256]{2,1,0:T(8,128)(2,1)} %prior_hbm.1, ...), custom_call_target="tpu_custom_call" | custom-call | tf_op jit(solution)/shard_map/step/pallas_call | solution.py:470
  33.0 0.0 copy-done
  33.0 0.0 copy-done.1
  33.0 1.5 %final.1 = (bf16[8,32,256]{2,1,0:T(8,128)(2,1)}, bf16[8,32,256]{2,1,0:T(8,128)(2,1)}, f32[8,64]{1,0:T(8,128)}, f32[9,64,64]{2,1,0:T(8,128)}, f32[8,64]{1,0:T(8,128)}) custom-call(f32[40,128]{1,0:T(8,128)S(1)} %get-tuple-element.13.tot_any, bf16[8,32,256]{2,1,0:T(8,128)(2,1)S(1)} %get-tuple-element.14.rem_any, ...), custom_call_target="tpu_custom_call" | custom-call | tf_op jit(solution)/shard_map/final/pallas_call | solution.py:500
Async XLA Ops:
  0.6 32.3 %copy-start = (bf16[9,64,64]{2,1,0:T(8,128)(2,1)S(1)}, bf16[9,64,64]{2,1,0:T(8,128)(2,1)}, u32[]{:S(2)}) copy-start(bf16[9,64,64]{2,1,0:T(8,128)(2,1)} %kern.1) | copy-start | bytes 221188
  0.6 32.3 %copy-start.1 = (bf16[8,64]{1,0:T(8,128)(2,1)S(1)}, bf16[8,64]{1,0:T(8,128)(2,1)}, u32[]{:S(2)}) copy-start(bf16[8,64]{1,0:T(8,128)(2,1)} %lift.1) | copy-start | bytes 3076
